TPU v7x, 256 devices: a whole 4x4x8 slice. The times are simulated.
256 devices in a mesh: rows: 64 (over x_hi, z, y), cols: 4 (over x_lo, core).
Axes of the slice: x: 4 (x_hi: 2, x_lo: 2; x = x_hi * 2 + x_lo), y: 4, z: 8, core: 2. Of those that a mesh axis runs over, the one named last changes fastest.
Arguments:
- features: bfloat16 [65536, 1024], P('rows', 'cols'), may hold values from -6 to 6
- targets: float32 [65536, 2048], P('rows', 'cols'), may hold values from -6 to 6
- block_index: int32 [2, 512], replicated, may hold values from 0 to 65535, as said below
Outputs:
- coefs: float32 [65536, 2048], P('rows', 'cols')
- residual: float32 [65536, 2048], P('rows', 'cols')
Inputs may be any that keep to these rules, and one draw needn't show every extreme that they name: `block_index`: the 2 x 512 indices are all distinct.
All inputs are finite; a program needn't handle non-finite values.
Results may differ from a plain program's by a relative error of at most 0.0003.
Values may be sent and summed in bfloat16 or wider, within the bound.
No kernel may reach another device: no remote copies, remote signals or barrier semaphores. Data moves between devices by JAX's collectives and lax.ppermute only.
A program may use at most 64 MiB of HBM per device.

v0:
```python
import jax
import jax.numpy as jnp
from jax import lax
from jax.sharding import Mesh
from jax.sharding import PartitionSpec as P

ROWS = ("rows_0", "rows_1", "rows_2")


ridge_value = 1.0


def padded_to(lines, length):
    spare = -len(lines) % length
    return jnp.pad(lines, [(0, spare)] + [(0, 0)] * (lines.ndim - 1))


def sent_to_all(value, axis):
    copies = jnp.broadcast_to(value, (lax.axis_size(axis), *value.shape))
    return lax.all_to_all(copies, axis, split_axis=0, concat_axis=0, tiled=True)


def laid_out(parts, dim):
    parts = jnp.moveaxis(parts, 0, dim)
    lengths = parts.shape
    return parts.reshape(*lengths[:dim], lengths[dim] * lengths[dim + 1], *lengths[dim + 2 :])


def gathered_by_axis(value, axes, dim):
    far, near = axes
    first = sent_to_all(value, far)
    parts = jnp.swapaxes(sent_to_all(first, near), 0, 1)
    return laid_out(parts.reshape(-1, *value.shape), dim)


def cut_along(value, dim, length):
    lengths = value.shape
    parts = value.reshape(*lengths[:dim], length, lengths[dim] // length, *lengths[dim + 1 :])
    return jnp.moveaxis(parts, dim, 0)


def sent_and_summed(value, axis, dim):
    parts = cut_along(value, dim, lax.axis_size(axis))
    arrived = lax.all_to_all(parts, axis, split_axis=0, concat_axis=0, tiled=True)
    return arrived.sum(axis=0)


def sum_in_two_steps(value, axes, dim):
    far, near = axes
    own = sent_and_summed(cut_along(value, dim, lax.axis_size(far)), near, dim + 1)
    return jnp.sum(lax.all_to_all(own, far, 0, 0, tiled=True), axis=0)


def total_of(value, axes):
    lines = value.reshape(-1, value.shape[-1])
    padded = padded_to(lines, lax.axis_size(axes[0]) * lax.axis_size(axes[1]))
    whole = gathered_by_axis(sum_in_two_steps(padded, axes, 0), axes, 0)
    return lax.slice_in_dim(whole, 0, len(lines)).reshape(value.shape)


def gathered_copies(value, axis, dim):
    return laid_out(sent_to_all(value, axis), dim)


def total_of_2(value, axes):
    lines = value.reshape(-1, value.shape[-1])
    own = sent_and_summed(padded_to(lines, lax.axis_size(axes)), axes, 0)
    whole = gathered_copies(own, axes, 0)
    return whole[: len(lines)].reshape(value.shape)


def pick_rows(select, values):
    return lax.dot_general(
        select, values, (((0,), (0,)), ((), ())), preferred_element_type=jnp.float32
    )


def pick_exact(select, values):
    return lax.dot_general(
        select,
        values,
        (((0,), (0,)), ((), ())),
        precision=lax.Precision.HIGHEST,
        preferred_element_type=jnp.float32,
    )


def kernel_from(gram, left_sq, right_sq, width):
    return jnp.exp(-(2.0 / width) * (left_sq[:, None] + right_sq[None, :] - 2.0 * gram))


def square_norms(states):
    return jnp.sum(jnp.square(states.astype(jnp.float32)), axis=1)


def fetch_rows(select, whole, values):
    select_half = select.astype(jnp.bfloat16)
    summed = total_of(pick_rows(select_half, whole), (("rows_0", "rows_1"), "rows_2"))
    points = summed.astype(jnp.bfloat16)
    picked = total_of_2(pick_exact(select, values), ROWS)
    return (points, picked)


def shards(features, targets, block_index):
    rows_here = features.shape[0]
    start = lax.axis_index(ROWS) * rows_here
    whole = gathered_copies(features, "cols", 1)
    width = whole.shape[1]
    local_sq = square_norms(whole)
    positions = start + lax.iota(jnp.int32, rows_here)
    coefs = jnp.zeros(targets.shape, jnp.float32)
    residual = targets
    block_size = block_index.shape[1]
    step_count = block_index.shape[0]
    earlier = []
    for step in range(step_count):
        select = (positions[:, None] == block_index[step][None, :]).astype(jnp.float32)
        points, picked = fetch_rows(select, whole, residual)
        point_sq = square_norms(points)
        gram = lax.dot_general(
            whole, points, (((1,), (1,)), ((), ())), preferred_element_type=jnp.float32
        )
        slab = kernel_from(gram, local_sq, point_sq, width)
        inner_gram = lax.dot_general(
            points, points, (((1,), (1,)), ((), ())), preferred_element_type=jnp.float32
        )
        inner = kernel_from(inner_gram, point_sq, point_sq, width)
        system = inner + ridge_value * jnp.eye(block_size, dtype=jnp.float32)
        factor = jnp.linalg.cholesky(system)
        delta = jax.scipy.linalg.cho_solve((factor, True), picked)
        earlier.append((points, point_sq, delta))
        coefs = coefs + jnp.dot(select, delta, precision=lax.Precision.HIGHEST)
        residual = residual - jnp.dot(
            slab + ridge_value * select, delta, precision=lax.Precision.HIGHEST
        )
    return (coefs, residual)


def solution(mesh):
    split = Mesh(
        mesh.devices.reshape(2, 8, 4, mesh.shape["cols"]), ("rows_0", "rows_1", "rows_2", "cols")
    )
    in_specs = (P(ROWS, "cols"), P(ROWS, "cols"), P())
    out_specs = (P(ROWS, "cols"), P(ROWS, "cols"))
    return jax.shard_map(
        shards, mesh=split, in_specs=in_specs, out_specs=out_specs, check_vma=False
    )
```

profile of v0, /device:TPU:6, one launch (start us, length us, event | category | flops | bytes accessed | tf_op | source)
XLA Modules:
  0.0 610.5 jit_solution(7404478503619211561)
XLA Ops:
  3.1 4.5 all-to-all-start
  7.7 4.5 fusion.43
  12.2 19.5 %all-to-all-done = bf16[4,1024,256]{2,1,0:T(8,128)(2,1)S(1)} async-done(((bf16[4,1024,256]{2,1,0:T(8,128)(2,1)}), bf16[4,1024,256]{2,1,0:T(8,128)(2,1)S(1)}, u32[]{:S(2)}, u32[]{:S(2)}) %all-to-all-start) | async-done | bytes 2097184 | tf_op jit(solution)/shard_map/all_to_all | solution.py:20
  31.7 14.7 %all-to-all-start.5 = ((f32[64,8,512]{2,1,0:T(8,128)}), f32[64,8,512]{2,1,0:T(8,128)S(1)}, u32[]{:S(2)}, u32[]{:S(2)}) async-start(f32[64,8,512]{2,1,0:T(8,128)} %fusion.43), calls=%async_computation.5 | async-start | bytes 2097152 | tf_op jit(solution)/shard_map/all_to_all | solution.py:44
  46.5 2.9 copy.22
  49.5 4.4 reshape.136
  58.2 15.1 %all-to-all-done.5 = f32[64,8,512]{2,1,0:T(8,128)S(1)} async-done(((f32[64,8,512]{2,1,0:T(8,128)}), f32[64,8,512]{2,1,0:T(8,128)S(1)}, u32[]{:S(2)}, u32[]{:S(2)}) %all-to-all-start.5) | async-done | bytes 1048608 | tf_op jit(solution)/shard_map/all_to_all | solution.py:44
  73.3 4.5 all-to-all-start.1
  77.9 2.9 fusion.31
  82.3 21.0 %all-to-all-done.1 = f32[4,16,8,1024]{3,2,1,0:T(8,128)} async-done(((f32[4,16,8,1024]{3,2,1,0:T(8,128)}), f32[4,16,8,1024]{3,2,1,0:T(8,128)}, u32[]{:S(2)}, u32[]{:S(2)}) %all-to-all-start.1) | async-done | bytes 2097184 | tf_op jit(solution)/shard_map/all_to_all | solution.py:44
  103.3 4.4 all-to-all-start.7
  110.4 21.6 %all-to-all-done.7 = f32[4,16,8,1024]{3,2,1,0:T(8,128)} async-done(((f32[4,16,8,1024]{3,2,1,0:T(8,128)}), f32[4,16,8,1024]{3,2,1,0:T(8,128)}, u32[]{:S(2)}, u32[]{:S(2)}) %all-to-all-start.7) | async-done | bytes 2097184 | tf_op jit(solution)/shard_map/all_to_all | solution.py:44
  132.0 8.8 %all-to-all-start.2 = ((f32[16,8,1024]{2,1,0:T(8,128)}), f32[16,8,1024]{2,1,0:T(8,128)}, u32[]{:S(2)}, u32[]{:S(2)}) async-start(f32[16,8,1024]{2,1,0:T(8,128)} %reduce_sum.81), calls=%async_computation.2 | async-start | bytes 1048576 | tf_op jit(solution)/shard_map/all_to_all | solution.py:51
  143.4 9.3 %all-to-all-done.2 = f32[16,8,1024]{2,1,0:T(8,128)} async-done(((f32[16,8,1024]{2,1,0:T(8,128)}), f32[16,8,1024]{2,1,0:T(8,128)}, u32[]{:S(2)}, u32[]{:S(2)}) %all-to-all-start.2) | async-done | bytes 524320 | tf_op jit(solution)/shard_map/all_to_all | solution.py:51
  152.7 7.1 %all-to-all-start.8 = ((f32[16,8,1024]{2,1,0:T(8,128)}), f32[16,8,1024]{2,1,0:T(8,128)}, u32[]{:S(2)}, u32[]{:S(2)}) async-start(f32[16,8,1024]{2,1,0:T(8,128)} %reduce_sum.85), calls=%async_computation.8 | async-start | bytes 1048576 | tf_op jit(solution)/shard_map/all_to_all | solution.py:51
  160.9 11.3 %all-to-all-done.8 = f32[16,8,1024]{2,1,0:T(8,128)} async-done(((f32[16,8,1024]{2,1,0:T(8,128)}), f32[16,8,1024]{2,1,0:T(8,128)}, u32[]{:S(2)}, u32[]{:S(2)}) %all-to-all-start.8) | async-done | bytes 524320 | tf_op jit(solution)/shard_map/all_to_all | solution.py:51
  172.9 7.1 %all-to-all-start.3 = ((bf16[16,8,1024]{2,1,0:T(8,128)(2,1)}), bf16[16,8,1024]{2,1,0:T(8,128)(2,1)S(1)}, u32[]{:S(2)}, u32[]{:S(2)}) async-start(bf16[16,8,1024]{2,1,0:T(8,128)(2,1)} %broadcast_in_dim.16), calls=%async_computation.3 | async-start | bytes 524288 | tf_op jit(solution)/shard_map/all_to_all | solution.py:20
  181.1 7.1 %all-to-all-done.3 = bf16[16,8,1024]{2,1,0:T(8,128)(2,1)S(1)} async-done(((bf16[16,8,1024]{2,1,0:T(8,128)(2,1)}), bf16[16,8,1024]{2,1,0:T(8,128)(2,1)S(1)}, u32[]{:S(2)}, u32[]{:S(2)}) %all-to-all-start.3) | async-done | bytes 262176 | tf_op jit(solution)/shard_map/all_to_all | solution.py:20
  188.2 14.4 %all_to_all.65 = bf16[16,8,1024]{2,1,0:T(8,128)(2,1)S(1)} all-to-all(bf16[16,8,1024]{2,1,0:T(8,128)(2,1)S(1)} %broadcast_in_dim.36), channel_id=1, replica_groups=mesh['rows_0'=2,'rows_1'=8,'rows_2'=4,'cols'=4] {'rows_0','rows_1'}, dimensions={0} | all-to-all | bytes 524288 | tf_op jit(solution)/shard_map/all_to_all | solution.py:20
  202.7 14.2 %all_to_all.66 = bf16[4,16,8,1024]{3,2,1,0:T(8,128)(2,1)} all-to-all(bf16[4,16,8,1024]{3,2,1,0:T(8,128)(2,1)S(1)} %broadcast_in_dim.37), channel_id=1, replica_groups=mesh['rows_0'=2,'rows_1'=8,'rows_2'=4,'cols'=4] {'rows_2'}, dimensions={0} | all-to-all | bytes 2097152 | tf_op jit(solution)/shard_map/all_to_all | solution.py:20
  218.0 4.3 all-to-all-start.4
  226.1 7.1 %all-to-all-done.4 = bf16[4,16,8,1024]{3,2,1,0:T(8,128)(2,1)} async-done(((bf16[4,16,8,1024]{3,2,1,0:T(8,128)(2,1)}), bf16[4,16,8,1024]{3,2,1,0:T(8,128)(2,1)}, u32[]{:S(2)}, u32[]{:S(2)}) %all-to-all-start.4) | async-done | bytes 1048608 | tf_op jit(solution)/shard_map/all_to_all | solution.py:20
  234.4 8.7 %all-to-all-start.6 = ((f32[64,8,512]{2,1,0:T(8,128)}), f32[64,8,512]{2,1,0:T(8,128)}, u32[]{:S(2)}, u32[]{:S(2)}) async-start(f32[64,8,512]{2,1,0:T(8,128)} %broadcast_in_dim.18), calls=%async_computation.6 | async-start | bytes 2097152 | tf_op jit(solution)/shard_map/all_to_all | solution.py:20
  248.0 11.7 %cholesky.358 = f32[128,128]{1,0:T(8,128)S(1)} custom-call(f32[128,128]{1,0:T(8,128)S(1)} %cholesky.439), custom_call_target="Cholesky" | custom-call | tf_op jit(solution)/shard_map/jit(cholesky)/cholesky | solution.py:129
  260.3 9.8 %custom-call.33 = f32[1,128,128]{1,2,0:T(8,128)S(1)} custom-call(f32[1,128,128]{2,1,0:T(8,128)S(1)} %get-tuple-element.55), custom_call_target="InvertDiagBlocksLowerTriangular" | custom-call | tf_op jit(solution)/shard_map/jit(cholesky)/cholesky | solution.py:129
  274.3 11.9 %cholesky.286 = f32[128,128]{1,0:T(8,128)S(1)} custom-call(f32[128,128]{1,0:T(8,128)S(1)} %cholesky.426), custom_call_target="Cholesky" | custom-call | tf_op jit(solution)/shard_map/jit(cholesky)/cholesky | solution.py:129
  286.2 9.8 %custom-call.29 = f32[1,128,128]{1,2,0:T(8,128)S(1)} custom-call(f32[1,128,128]{2,1,0:T(8,128)S(1)} %get-tuple-element.65), custom_call_target="InvertDiagBlocksLowerTriangular" | custom-call | tf_op jit(solution)/shard_map/jit(cholesky)/cholesky | solution.py:129
  298.7 11.7 %cholesky.305 = f32[128,128]{1,0:T(8,128)S(1)} custom-call(f32[128,128]{1,0:T(8,128)S(1)} %cholesky.430), custom_call_target="Cholesky" | custom-call | tf_op jit(solution)/shard_map/jit(cholesky)/cholesky | solution.py:129
  310.4 9.8 %custom-call.30 = f32[1,128,128]{1,2,0:T(8,128)S(1)} custom-call(f32[1,128,128]{2,1,0:T(8,128)S(1)} %get-tuple-element.62), custom_call_target="InvertDiagBlocksLowerTriangular" | custom-call | tf_op jit(solution)/shard_map/jit(cholesky)/cholesky | solution.py:129
  321.8 12.1 %cholesky.326 = f32[128,128]{1,0:T(8,128)S(1)} custom-call(f32[128,128]{1,0:T(8,128)S(1)} %cholesky.435), custom_call_target="Cholesky" | custom-call | tf_op jit(solution)/shard_map/jit(cholesky)/cholesky | solution.py:129
  333.9 9.8 %custom-call.31 = f32[1,128,128]{1,2,0:T(8,128)S(1)} custom-call(f32[1,128,128]{2,1,0:T(8,128)S(1)} %get-tuple-element.59), custom_call_target="InvertDiagBlocksLowerTriangular" | custom-call | tf_op jit(solution)/shard_map/jit(cholesky)/cholesky | solution.py:129
  345.2 11.7 %cholesky.343 = f32[128,128]{1,0:T(8,128)S(1)} custom-call(f32[128,128]{1,0:T(8,128)S(1)} %convolution_subtract_fusion.17), custom_call_target="Cholesky" | custom-call | tf_op jit(solution)/shard_map/jit(cholesky)/cholesky | solution.py:129
  361.6 7.8 %while.4 = (s32[]{:T(128)}, f32[512,512]{1,0:T(8,128)S(1)}, s32[4,2]{0,1:T(2,128)S(1)}, f32[4,128,128]{2,1,0:T(8,128)S(1)}, s32[]{:T(128)}) while((s32[]{:T(128)}, f32[512,512]{1,0:T(8,128)S(1)}, s32[4,2]{0,1:T(2,128)S(1)}, f32[4,128,128]{2,1,0:T(8,128)S(1)}, s32[]{:T(128)}) %tuple.61), condition=%wide.while_cond, body=%wide.while_body.sunk | while | flops 2 | bytes 131189 | solution.py:130
  369.4 39.5 %custom-call.32 = f32[4,128,128]{1,2,0:T(8,128)S(1)} custom-call(f32[4,128,128]{2,1,0:T(8,128)S(1)} %get-tuple-element.18), custom_call_target="InvertDiagBlocksLowerTriangular" | custom-call | tf_op jit(solution)/shard_map/jit(_cho_solve)/triangular_solve | solution.py:130
  420.7 4.1 fusion.40
  424.8 3.1 fusion.46
  428.0 13.0 %all-to-all-start.11 = ((f32[64,8,512]{2,1,0:T(8,128)}), f32[64,8,512]{2,1,0:T(8,128)}, u32[]{:S(2)}, u32[]{:S(2)}) async-start(f32[64,8,512]{2,1,0:T(8,128)} %fusion.46), calls=%async_computation.11 | async-start | bytes 2097152 | tf_op jit(solution)/shard_map/all_to_all | solution.py:44
  444.1 11.7 %cholesky.377 = f32[128,128]{1,0:T(8,128)S(1)} custom-call(f32[128,128]{1,0:T(8,128)S(1)} %cholesky.443), custom_call_target="Cholesky" | custom-call | tf_op jit(solution)/shard_map/jit(cholesky)/cholesky | solution.py:129
  456.4 9.8 %custom-call.34 = f32[1,128,128]{1,2,0:T(8,128)S(1)} custom-call(f32[1,128,128]{2,1,0:T(8,128)S(1)} %get-tuple-element.52), custom_call_target="InvertDiagBlocksLowerTriangular" | custom-call | tf_op jit(solution)/shard_map/jit(cholesky)/cholesky | solution.py:129
  469.3 13.2 %cholesky.398 = f32[128,128]{1,0:T(8,128)} custom-call(f32[128,128]{1,0:T(8,128)} %cholesky.448), custom_call_target="Cholesky" | custom-call | tf_op jit(solution)/shard_map/jit(cholesky)/cholesky | solution.py:129
  484.5 11.7 %custom-call.35 = f32[1,128,128]{1,2,0:T(8,128)} custom-call(f32[1,128,128]{2,1,0:T(8,128)} %get-tuple-element.49), custom_call_target="InvertDiagBlocksLowerTriangular" | custom-call | tf_op jit(solution)/shard_map/jit(cholesky)/cholesky | solution.py:129
  498.5 11.7 %cholesky.415 = f32[128,128]{1,0:T(8,128)S(1)} custom-call(f32[128,128]{1,0:T(8,128)S(1)} %convolution_subtract_fusion.16), custom_call_target="Cholesky" | custom-call | tf_op jit(solution)/shard_map/jit(cholesky)/cholesky | solution.py:129
  517.0 13.0 %all-to-all-start.12 = ((f32[64,8,512]{2,1,0:T(8,128)}), f32[64,8,512]{2,1,0:T(8,128)}, u32[]{:S(2)}, u32[]{:S(2)}) async-start(f32[64,8,512]{2,1,0:T(8,128)} %broadcast_in_dim.38), calls=%async_computation.12 | async-start | bytes 2097152 | tf_op jit(solution)/shard_map/all_to_all | solution.py:20
  532.4 11.4 %while.5 = (s32[]{:T(128)}, f32[512,512]{1,0:T(8,128)}, s32[4,2]{0,1:T(2,128)S(1)}, f32[4,128,128]{2,1,0:T(8,128)S(1)}, s32[]{:T(128)}) while((s32[]{:T(128)}, f32[512,512]{1,0:T(8,128)}, s32[4,2]{0,1:T(2,128)S(1)}, f32[4,128,128]{2,1,0:T(8,128)S(1)}, s32[]{:T(128)}) %tuple.67), condition=%wide.while_cond.clone, body=%wide.while_body.clone.sunk | while | flops 2 | bytes 131189 | solution.py:130
  543.9 40.1 %custom-call.36 = f32[4,128,128]{1,2,0:T(8,128)} custom-call(f32[4,128,128]{2,1,0:T(8,128)S(1)} %get-tuple-element.19), custom_call_target="InvertDiagBlocksLowerTriangular" | custom-call | tf_op jit(solution)/shard_map/jit(_cho_solve)/triangular_solve | solution.py:130
  584.0 4.6 fusion.184
  601.6 5.4 fusion.37
  607.0 3.3 fusion.34
  (171 shorter events, 101.6 us)
Async XLA Ops:
  3.1 4.5 copy-start.20
  3.1 28.6 %all-to-all-start = ((bf16[4,1024,256]{2,1,0:T(8,128)(2,1)}), bf16[4,1024,256]{2,1,0:T(8,128)(2,1)S(1)}, u32[]{:S(2)}, u32[]{:S(2)}) async-start(bf16[4,1024,256]{2,1,0:T(8,128)(2,1)} %broadcast_in_dim.15), calls=%async_computation | async-start | bytes 4194304 | tf_op jit(solution)/shard_map/all_to_all | solution.py:20
  7.7 417.1 %copy-start.18 = (s32[1,512]{1,0:T(1,128)}, s32[1,512]{1,0:T(1,128)S(1)}, u32[]{:S(2)}) copy-start(s32[1,512]{1,0:T(1,128)S(1)} %get-tuple-element.67) | copy-start | bytes 6148
  31.7 41.6 %all-to-all-start.5 = ((f32[64,8,512]{2,1,0:T(8,128)}), f32[64,8,512]{2,1,0:T(8,128)S(1)}, u32[]{:S(2)}, u32[]{:S(2)}) async-start(f32[64,8,512]{2,1,0:T(8,128)} %fusion.43), calls=%async_computation.5 | async-start | bytes 2097152 | tf_op jit(solution)/shard_map/all_to_all | solution.py:44
  73.3 30.0 %all-to-all-start.1 = ((f32[4,16,8,1024]{3,2,1,0:T(8,128)}), f32[4,16,8,1024]{3,2,1,0:T(8,128)}, u32[]{:S(2)}, u32[]{:S(2)}) async-start(f32[4,16,8,1024]{3,2,1,0:T(8,128)} %copy.23), calls=%async_computation.1 | async-start | bytes 4194304 | tf_op jit(solution)/shard_map/all_to_all | solution.py:44
  103.3 28.7 %all-to-all-start.7 = ((f32[4,16,8,1024]{3,2,1,0:T(8,128)}), f32[4,16,8,1024]{3,2,1,0:T(8,128)}, u32[]{:S(2)}, u32[]{:S(2)}) async-start(f32[4,16,8,1024]{3,2,1,0:T(8,128)} %copy.27), calls=%async_computation.7 | async-start | bytes 4194304 | tf_op jit(solution)/shard_map/all_to_all | solution.py:44
  132.0 20.7 %all-to-all-start.2 = ((f32[16,8,1024]{2,1,0:T(8,128)}), f32[16,8,1024]{2,1,0:T(8,128)}, u32[]{:S(2)}, u32[]{:S(2)}) async-start(f32[16,8,1024]{2,1,0:T(8,128)} %reduce_sum.81), calls=%async_computation.2 | async-start | bytes 1048576 | tf_op jit(solution)/shard_map/all_to_all | solution.py:51
  152.7 19.5 %all-to-all-start.8 = ((f32[16,8,1024]{2,1,0:T(8,128)}), f32[16,8,1024]{2,1,0:T(8,128)}, u32[]{:S(2)}, u32[]{:S(2)}) async-start(f32[16,8,1024]{2,1,0:T(8,128)} %reduce_sum.85), calls=%async_computation.8 | async-start | bytes 1048576 | tf_op jit(solution)/shard_map/all_to_all | solution.py:51
  172.9 15.3 %all-to-all-start.3 = ((bf16[16,8,1024]{2,1,0:T(8,128)(2,1)}), bf16[16,8,1024]{2,1,0:T(8,128)(2,1)S(1)}, u32[]{:S(2)}, u32[]{:S(2)}) async-start(bf16[16,8,1024]{2,1,0:T(8,128)(2,1)} %broadcast_in_dim.16), calls=%async_computation.3 | async-start | bytes 524288 | tf_op jit(solution)/shard_map/all_to_all | solution.py:20
  218.0 15.2 %all-to-all-start.4 = ((bf16[4,16,8,1024]{3,2,1,0:T(8,128)(2,1)}), bf16[4,16,8,1024]{3,2,1,0:T(8,128)(2,1)}, u32[]{:S(2)}, u32[]{:S(2)}) async-start(bf16[4,16,8,1024]{3,2,1,0:T(8,128)(2,1)} %broadcast_in_dim.17), calls=%async_computation.4 | async-start | bytes 2097152 | tf_op jit(solution)/shard_map/all_to_all | solution.py:20
  226.0 19.5 %copy-start.13 = (bf16[4,16,8,1024]{3,2,0,1:T(8,128)(2,1)}, bf16[4,16,8,1024]{3,2,0,1:T(8,128)(2,1)S(1)}, u32[]{:S(2)}) copy-start(bf16[4,16,8,1024]{3,2,0,1:T(8,128)(2,1)S(1)} %get-tuple-element.39) | copy-start | bytes 3145732
  226.1 19.4 %copy-start.16 = (f32[512]{0:T(512)}, f32[512]{0:T(512)S(1)}, u32[]{:S(2)}) copy-start(f32[512]{0:T(512)S(1)} %add.128) | copy-start | bytes 6148
  234.4 174.5 %all-to-all-start.6 = ((f32[64,8,512]{2,1,0:T(8,128)}), f32[64,8,512]{2,1,0:T(8,128)}, u32[]{:S(2)}, u32[]{:S(2)}) async-start(f32[64,8,512]{2,1,0:T(8,128)} %broadcast_in_dim.18), calls=%async_computation.6 | async-start | bytes 2097152 | tf_op jit(solution)/shard_map/all_to_all | solution.py:20
  247.0 1.0 copy-start.5
  273.3 1.0 copy-start.6
  416.7 2.3 copy-start.9
  416.7 2.3 copy-start.14
  417.1 3.3 copy-start
  417.9 2.4 copy-start.3
  419.0 1.4 copy-start.7
  419.0 1.7 copy-start.10
  428.0 86.6 %all-to-all-start.11 = ((f32[64,8,512]{2,1,0:T(8,128)}), f32[64,8,512]{2,1,0:T(8,128)}, u32[]{:S(2)}, u32[]{:S(2)}) async-start(f32[64,8,512]{2,1,0:T(8,128)} %fusion.46), calls=%async_computation.11 | async-start | bytes 2097152 | tf_op jit(solution)/shard_map/all_to_all | solution.py:44
  443.5 0.7 copy-start.15
  517.0 71.6 %all-to-all-start.12 = ((f32[64,8,512]{2,1,0:T(8,128)}), f32[64,8,512]{2,1,0:T(8,128)}, u32[]{:S(2)}, u32[]{:S(2)}) async-start(f32[64,8,512]{2,1,0:T(8,128)} %broadcast_in_dim.38), calls=%async_computation.12 | async-start | bytes 2097152 | tf_op jit(solution)/shard_map/all_to_all | solution.py:20
  584.0 6.1 copy-start.2
  588.6 5.4 copy-start.12
  597.3 2.3 copy-start.19
  599.2 2.4 copy-start.11
  599.2 2.4 copy-start.17
  601.6 5.4 copy-start.1
  601.6 5.4 copy-start.4
  601.6 5.4 copy-start.8
where the time goes:
time: 622 us; the launch traced here: 610 us
  other arithmetic  259 us (42%)
  waiting for transfers between devices  112 us (18%)
  starting transfers between devices  90.1 us (14%)
  matrix products  70.8 us (11%)
  local copies, waits for them, and re-layouts  42.8 us (7%)
  blocking collectives  28.6 us (5%)
  between operations  6.59 us (1%)
    another operation x28, other arithmetic, shards(): factor = jnp.linalg.cholesky(system)  165 us
    another operation x5, other arithmetic, shards(): delta = jax.scipy.linalg.cho_solve((factor, True), picked)  80.8 us
    all_to_all x4, waiting for transfers between devices, sent_and_summed(): lax.all_to_all(parts, axis, split_axis=0, concat_axis=0, tiled=True)  57.7 us
    all_to_all x5, starting transfers between devices, sent_to_all(): return lax.all_to_all(copies, axis, split_axis=0, concat_axis=0, tiled=True)  37.6 us
    all_to_all x4, starting transfers between devices, sent_and_summed(): lax.all_to_all(parts, axis, split_axis=0, concat_axis=0, tiled=True)  36.7 us
    all_to_all x5, waiting for transfers between devices, sent_to_all(): return lax.all_to_all(copies, axis, split_axis=0, concat_axis=0, tiled=True)  33.7 us
    all_to_all x2, blocking collectives, sent_to_all(): return lax.all_to_all(copies, axis, split_axis=0, concat_axis=0, tiled=True)  28.6 us
    another operation x28, matrix products, shards(): delta = jax.scipy.linalg.cho_solve((factor, True), picked)  20.7 us
  transfers between devices with their start and end apart: 11, of which 8 were waited for; matrix products, arithmetic and copies ran while one was open for 53% of the time, Pallas kernels for 0%

commit v1 on v0

v1 whole, which is shorter than its diff:
```python
import functools

import jax
import jax.numpy as jnp
from jax import lax
from jax.experimental import pallas as pl
from jax.experimental.pallas import tpu as pltpu
from jax.sharding import Mesh
from jax.sharding import PartitionSpec as P

ROWS = ("r0", "r1", "r2")
COLS = ("xlo", "core")
RIDGE = 1.0
LEAF = 128
HI = lax.Precision.HIGHEST
SWAP = [(0, 1), (1, 0)]


def mm(a, b):
    return lax.dot_general(a, b, (((1,), (0,)), ((), ())), precision=HI, preferred_element_type=jnp.float32)


def mm_nt(a, b):
    return lax.dot_general(a, b, (((1,), (1,)), ((), ())), preferred_element_type=jnp.float32)


def inv2(a, b, d):
    i = 1.0 / (a * d - b * b)
    return d * i, -b * i, a * i


def leaf_inverse(m):
    n = m.shape[-1]
    lane = lax.broadcasted_iota(jnp.int32, (1, 1, n), 2)
    sub = lax.broadcasted_iota(jnp.int32, (1, n, 1), 1)
    for j in range(0, n, 4):
        c = [jnp.broadcast_to(m[:, :, j + q : j + q + 1], m.shape) for q in range(4)]
        e = lambda p, q: c[q][:, j + p : j + p + 1, :]
        r = []
        for q in range(4):
            row = m[:, j + q : j + q + 1, :]
            for w in range(4):
                row = jnp.where(lane == j + w, 1.0 if w == q else 0.0, row)
            r.append(row)
        x11, x12, x22 = inv2(e(0, 0), e(0, 1), e(1, 1))
        b = [[e(0, 2), e(0, 3)], [e(1, 2), e(1, 3)]]
        y = [
            [x11 * b[0][q] + x12 * b[1][q] for q in range(2)],
            [x12 * b[0][q] + x22 * b[1][q] for q in range(2)],
        ]
        s = lambda p, q, base: base - (b[0][p] * y[0][q] + b[1][p] * y[1][q])
        z11, z12, z22 = inv2(s(0, 0, e(2, 2)), s(0, 1, e(2, 3)), s(1, 1, e(3, 3)))
        w0 = x11 * r[0] + x12 * r[1]
        w1 = x12 * r[0] + x22 * r[1]
        t0 = r[2] - (b[0][0] * w0 + b[1][0] * w1)
        t1 = r[3] - (b[0][1] * w0 + b[1][1] * w1)
        s2 = z11 * t0 + z12 * t1
        s3 = z12 * t0 + z22 * t1
        s0 = w0 - (y[0][0] * s2 + y[0][1] * s3)
        s1 = w1 - (y[1][0] * s2 + y[1][1] * s3)
        new = jnp.where((lane >= j) & (lane < j + 4), 0.0, m)
        new = new - ((c[0] * s0 + c[1] * s1) + (c[2] * s2 + c[3] * s3))
        for q, sq in enumerate((s0, s1, s2, s3)):
            new = jnp.where(sub == j + q, sq, new)
        m = new
    return m


def pick_points_kernel(idx_ref, f_ref, o_ref):
    n = f_ref.shape[0]
    sel = (idx_ref[...] == lax.broadcasted_iota(jnp.int32, (idx_ref.shape[0], n), 1)).astype(jnp.bfloat16)
    o_ref[...] = jnp.dot(sel, f_ref[...], preferred_element_type=jnp.float32).astype(jnp.bfloat16)


def split3(x):
    hi = x.astype(jnp.bfloat16)
    rest = x - hi.astype(jnp.float32)
    mid = rest.astype(jnp.bfloat16)
    low = (rest - mid.astype(jnp.float32)).astype(jnp.bfloat16)
    return hi, mid, low


def pick_targets_kernel(idx_ref, t_ref, o_ref, parts):
    n, w = t_ref.shape

    @pl.when(pl.program_id(0) == 0)
    def _():
        for i, part in enumerate(split3(t_ref[...])):
            parts[:, i * w : (i + 1) * w] = part

    sel = (idx_ref[...] == lax.broadcasted_iota(jnp.int32, (idx_ref.shape[0], n), 1)).astype(jnp.bfloat16)
    got = jnp.dot(sel, parts[...], preferred_element_type=jnp.float32)
    o_ref[...] = (got[:, :w] + got[:, w : 2 * w]) + got[:, 2 * w :]


def factor_kernel(p0, p1, p2, p3, w_ref, pn_ref, a_ref, r_ref, *, width):
    points = (p0, p1, p2, p3)
    n = p0.shape[0] // 2
    gram = lambda a, b: sum(mm_nt(p[a * n : (a + 1) * n, :], p[b * n : (b + 1) * n, :]) for p in points)
    eye = lax.broadcasted_iota(jnp.int32, (n, n), 0) == lax.broadcasted_iota(jnp.int32, (n, n), 1)
    scale = -(2.0 / width)
    rows, cols = [], []
    for s in range(2):
        g = gram(s, s)
        diag = jnp.where(eye, g, 0.0)
        rows.append(jnp.sum(diag, axis=0, keepdims=True))
        cols.append(jnp.sum(diag, axis=1, keepdims=True))
        k = jnp.exp(scale * (cols[s] + rows[s] - 2.0 * g))
        a_ref[s] = k + jnp.where(eye, RIDGE, 0.0)
        pn_ref[:, s * n : (s + 1) * n] = jnp.broadcast_to(rows[s], (8, n))
    w_ref[n:, :n] = jnp.exp(scale * (cols[1] + rows[0] - 2.0 * gram(1, 0)))
    w_ref[:n, n:] = jnp.zeros((n, n), jnp.float32)

    def step(k, carry):
        at = pl.ds(pl.multiple_of(k * LEAF, LEAF), LEAF)
        dinv = leaf_inverse(a_ref[:, at, at])
        for s in range(2):
            r_ref[s] = mm(dinv[s], a_ref[s, at, :])
            r_ref[s, :, at] = dinv[s]
            col = a_ref[s, :, at]
            a_ref[s, :, at] = jnp.zeros((n, LEAF), jnp.float32)
            a_ref[s] = a_ref[s] - mm(col, r_ref[s])
            a_ref[s, at, :] = r_ref[s]
        return carry

    lax.fori_loop(0, n // LEAF, step, 0)
    w_ref[:n, :n] = a_ref[0]
    w_ref[n:, n:] = a_ref[1]
    w_ref[n:, :n] = -mm(a_ref[1], mm(w_ref[n:, :n], a_ref[0]))


def response_kernel(f0, f1, f2, f3, p0, p1, p2, p3, pn_ref, w_ref, v_ref, *, width):
    g = None
    sq = None
    for f, p in ((f0, p0), (f1, p1), (f2, p2), (f3, p3)):
        x = f[...]
        part = mm_nt(x, p[...])
        g = part if g is None else g + part
        xf = x.astype(jnp.float32)
        xs = xf * xf
        sq = xs if sq is None else sq + xs
    n = w_ref.shape[0] // 2
    slab = jnp.exp(-(2.0 / width) * (jnp.sum(sq, axis=1, keepdims=True) + pn_ref[0:1, :] - 2.0 * g))
    v_ref[:, :n] = mm(slab, w_ref[:, :n])
    v_ref[:, n:] = mm(slab[:, n:], w_ref[n:, n:])


def tail_kernel(idx_ref, t_ref, v_ref, w_ref, tp_ref, c_ref, r_ref, parts):
    n, w = tp_ref.shape
    rows = t_ref.shape[0]

    @pl.when(pl.program_id(0) == 0)
    def _():
        delta = mm(w_ref[...], tp_ref[...])
        for i, part in enumerate(split3(delta)):
            parts[:, i * w : (i + 1) * w] = part

    row = lax.broadcasted_iota(jnp.int32, (rows, n), 0) + pl.program_id(0) * rows
    sel = (idx_ref[0:1, :] == row).astype(jnp.bfloat16)
    got = jnp.dot(sel, parts[...], preferred_element_type=jnp.float32)
    coefs = (got[:, :w] + got[:, w : 2 * w]) + got[:, 2 * w :]
    c_ref[...] = coefs
    r_ref[...] = t_ref[...] - mm(v_ref[...], tp_ref[...]) - RIDGE * coefs


def full(shape):
    return pl.BlockSpec(shape, lambda i: (0,) * len(shape))


def tile(rows, width):
    return pl.BlockSpec((rows, width), lambda i: (i, 0))


def pick_points(idx_col, f):
    m, n, w = idx_col.shape[0], *f.shape
    bm = 256
    return pl.pallas_call(
        pick_points_kernel,
        grid=(m // bm,),
        in_specs=[tile(bm, 1), full((n, w))],
        out_specs=tile(bm, w),
        out_shape=jax.ShapeDtypeStruct((m, w), jnp.bfloat16),
        name="pick_points",
    )(idx_col, f)


def pick_targets(idx_col, t):
    m, n, w = idx_col.shape[0], *t.shape
    bm = 256
    return pl.pallas_call(
        pick_targets_kernel,
        grid=(m // bm,),
        in_specs=[tile(bm, 1), full((n, w))],
        out_specs=tile(bm, w),
        out_shape=jax.ShapeDtypeStruct((m, w), jnp.float32),
        scratch_shapes=[pltpu.VMEM((n, 3 * w), jnp.bfloat16)],
        name="pick_targets",
        cost_estimate=pl.CostEstimate(flops=6 * m * n * w, transcendentals=0, bytes_accessed=8 * n * w),
    )(idx_col, t)


def factor(points, width):
    m = points[0].shape[0]
    n = m // 2
    return pl.pallas_call(
        functools.partial(factor_kernel, width=width),
        out_shape=(jax.ShapeDtypeStruct((m, m), jnp.float32), jax.ShapeDtypeStruct((8, m), jnp.float32)),
        scratch_shapes=[pltpu.VMEM((2, n, n), jnp.float32), pltpu.VMEM((2, LEAF, n), jnp.float32)],
        name="factor",
        cost_estimate=pl.CostEstimate(flops=40 * 10**9, transcendentals=0, bytes_accessed=8 * m * m),
    )(*points)


def response(own, points, pn, w, width):
    n = own[0].shape[0]
    m = w.shape[0]
    bm = 256
    return pl.pallas_call(
        functools.partial(response_kernel, width=width),
        grid=(n // bm,),
        in_specs=[tile(bm, x.shape[1]) for x in own]
        + [full(x.shape) for x in points]
        + [full(pn.shape), full(w.shape)],
        out_specs=tile(bm, m),
        out_shape=jax.ShapeDtypeStruct((n, m), jnp.float32),
        name="response",
        cost_estimate=pl.CostEstimate(flops=12 * n * m * m, transcendentals=0, bytes_accessed=8 * m * m),
    )(*own, *points, pn, w)


def tail(idx_row, t, v, w, tp):
    n, width = t.shape
    m = w.shape[0]
    bm = 256
    return pl.pallas_call(
        tail_kernel,
        grid=(n // bm,),
        in_specs=[full(idx_row.shape), tile(bm, width), tile(bm, m), full(w.shape), full(tp.shape)],
        out_specs=(tile(bm, width), tile(bm, width)),
        out_shape=(jax.ShapeDtypeStruct(t.shape, jnp.float32),) * 2,
        scratch_shapes=[pltpu.VMEM((m, 3 * width), jnp.bfloat16)],
        name="tail",
    )(idx_row, t, v, w, tp)


def exchange(parts):
    return lax.all_to_all(parts, ROWS, split_axis=0, concat_axis=0, tiled=True)


def scattered_sum(x, count):
    parts = exchange(x.reshape(count, x.shape[0] // count, x.shape[1]))
    return parts.sum(axis=0)


def gathered(x, count):
    parts = exchange(jnp.broadcast_to(x, (count, *x.shape)))
    return parts.reshape(-1, x.shape[1])


def over_cols(x):
    other = lax.ppermute(x, "xlo", SWAP)
    return (x, other, lax.ppermute(x, "core", SWAP), lax.ppermute(other, "core", SWAP))


def shards(features, targets, block_index):
    rows_here = features.shape[0]
    count = lax.axis_size(ROWS)
    width = features.shape[1] * lax.axis_size(COLS)
    start = lax.axis_index(ROWS) * rows_here
    idx = block_index.reshape(-1) - start
    idx_col = idx[:, None]
    idx_row = jnp.broadcast_to(idx[None, :], (8, idx.shape[0]))
    own = over_cols(features)
    p = gathered(scattered_sum(pick_points(idx_col, features), count), count)
    t = pick_targets(idx_col, targets)
    t, p = lax.optimization_barrier((t, p))
    points = over_cols(p)
    tp = gathered(scattered_sum(t, count), count)
    w, pn = factor(points, width)
    v = response(own, points, pn, w, width)
    return tail(idx_row, targets, v, w, tp)


def solution(mesh):
    split = Mesh(mesh.devices.reshape(2, 8, 4, 2, 2), ROWS + COLS)
    return jax.shard_map(
        shards,
        mesh=split,
        in_specs=(P(ROWS, COLS), P(ROWS, COLS), P()),
        out_specs=(P(ROWS, COLS), P(ROWS, COLS)),
        check_vma=False,
    )
```

time: 622 us -> 226 us (0.36); the launches traced: 610 us -> 223 us
  other arithmetic: 259 us -> 0.93 us
  Pallas kernels: 0 us -> 102 us
  matrix products: 70.8 us -> 0 us
  starting transfers between devices: 90.1 us -> 29.7 us
  waiting for transfers between devices: 112 us -> 53.8 us
  local copies, waits for them, and re-layouts: 42.8 us -> 4.82 us
    another operation x33 -> x0, other arithmetic: 246 us -> none  [the longest x28 165 us: shards(): factor = jnp.linalg.cholesky(system)]
    pallas_call x0 -> x5, Pallas kernels: none -> 102 us  [the longest x1 51.1 us: factor(): pl.pallas_call(functools.partial(factor_kernel, width=width), out_shape=(...]
    all_to_all x11 -> x3, waiting for transfers between devices: 112 us -> 13.6 us  [exchange(): return lax.all_to_all(parts, ROWS, split_axis=0, concat_axis=0, tiled=True)]
    all_to_all x11 -> x3, starting transfers between devices: 90.1 us -> 27.1 us  [exchange(): return lax.all_to_all(parts, ROWS, split_axis=0, concat_axis=0, tiled=True)]
    ppermute x0 -> x6, waiting for transfers between devices: none -> 40.1 us  [the longest x2 40.1 us: over_cols(): other = lax.ppermute(x, 'xlo', SWAP)]
    dot_general x12 -> x0, matrix products: 37.4 us -> none  [the longest x2 9.48 us: shards(): jnp.dot(slab + ridge_value * select, delta, precision=lax.Precision.HIGHEST)]
    another operation x40 -> x0, matrix products: 33.4 us -> none  [the longest x28 20.7 us: shards(): delta = jax.scipy.linalg.cho_solve((factor, True), picked)]
    another operation x35 -> x0, local copies, waits for them, and re-layouts: 20 us -> none  [the longest x27 19.2 us: shards(): delta = jax.scipy.linalg.cho_solve((factor, True), picked)]
  transfers between devices with their start and end apart: 11 -> 9, of which waited for: 8 -> 4; matrix products, arithmetic and copies ran while one was open for 53% -> 1% of each run, Pallas kernels for 0% -> 34%
where the time goes in v1:
time: 226 us; the launch traced here: 223 us
  Pallas kernels  102 us (45%)
  waiting for transfers between devices  53.8 us (24%)
  blocking collectives  31 us (14%)
  starting transfers between devices  29.7 us (13%)
  local copies, waits for them, and re-layouts  4.82 us (2%)
    pallas_call x1, Pallas kernels, factor(): pl.pallas_call(functools.partial(factor_kernel, width=width), out_shape=(...  51.1 us
    ppermute x2, waiting for transfers between devices, over_cols(): other = lax.ppermute(x, 'xlo', SWAP)  40.1 us
    all_to_all x1, blocking collectives, exchange(): return lax.all_to_all(parts, ROWS, split_axis=0, concat_axis=0, tiled=True)  31 us
    all_to_all x3, starting transfers between devices, exchange(): return lax.all_to_all(parts, ROWS, split_axis=0, concat_axis=0, tiled=True)  27.1 us
    pallas_call x1, Pallas kernels, tail(): pl.pallas_call(tail_kernel, grid=(n // bm,), in_specs=[full(idx_row.shape...  21.9 us
    pallas_call x1, Pallas kernels, response(): pl.pallas_call(functools.partial(response_kernel, width=width), grid=(n /...  18 us
    all_to_all x3, waiting for transfers between devices, exchange(): return lax.all_to_all(parts, ROWS, split_axis=0, concat_axis=0, tiled=True)  13.6 us
    pallas_call x1, Pallas kernels, pick_targets(): pl.pallas_call(pick_targets_kernel, grid=(m // bm,), in_specs=[tile(bm, 1...  7.31 us
  transfers between devices with their start and end apart: 9, of which 4 were waited for; matrix products, arithmetic and copies ran while one was open for 1% of the time, Pallas kernels for 34%

profile of v1, /device:TPU:6, one launch (start us, length us, event | category | flops | bytes accessed | tf_op | source)
XLA Modules:
  0.0 223.3 jit_solution(8735540944258649057)
XLA Ops:
  0.6 0.7 subtract_bitcast_fusion
  1.3 1.0 copy.9
  2.4 4.1 %pick_points.1 = bf16[1024,256]{1,0:T(8,128)(2,1)} custom-call(s32[1024,1]{1,0:T(8,128)} %bitcast.13, bf16[1024,256]{1,0:T(8,128)(2,1)} %f0.1), custom_call_target="tpu_custom_call" | custom-call | tf_op jit(solution)/shard_map/pick_points/pallas_call | solution.py:177
  6.5 31.0 %all_to_all.20 = bf16[64,16,256]{2,1,0:T(8,128)(2,1)S(1)} all-to-all(bf16[64,16,256]{2,1,0:T(8,128)(2,1)} %bitcast.15), channel_id=1, replica_groups=mesh['r0'=2,'r1'=8,'r2'=4,'xlo'=2,'core'=2] {'r0','r1','r2'}, dimensions={0} | all-to-all | bytes 1048576 | tf_op jit(solution)/shard_map/all_to_all | solution.py:247
  37.5 0.1 reduce_sum.21
  37.6 0.8 broadcast_in_dim.14
  38.4 8.9 %all-to-all-start.1 = ((bf16[64,16,256]{2,1,0:T(8,128)(2,1)}), bf16[64,16,256]{2,1,0:T(8,128)(2,1)S(1)}, u32[]{:S(2)}, u32[]{:S(2)}) async-start(bf16[64,16,256]{2,1,0:T(8,128)(2,1)} %broadcast_in_dim.14), calls=%async_computation.1 | async-start | bytes 1048576 | tf_op jit(solution)/shard_map/all_to_all | solution.py:247
  47.3 7.3 %pick_targets.1 = f32[1024,512]{1,0:T(8,128)} custom-call(s32[1024,1]{1,0:T(8,128)} %bitcast.14, f32[1024,512]{1,0:T(8,128)} %t_ref.3), custom_call_target="tpu_custom_call" | custom-call | flops 3221225472 | bytes 4194304 | tf_op jit(solution)/shard_map/pick_targets/pallas_call | solution.py:190
  54.6 8.5 %all-to-all-done.1 = bf16[64,16,256]{2,1,0:T(8,128)(2,1)S(1)} async-done(((bf16[64,16,256]{2,1,0:T(8,128)(2,1)}), bf16[64,16,256]{2,1,0:T(8,128)(2,1)S(1)}, u32[]{:S(2)}, u32[]{:S(2)}) %all-to-all-start.1) | async-done | bytes 524320 | tf_op jit(solution)/shard_map/all_to_all | solution.py:247
  63.1 0.0 copy-start.2
  63.1 0.0 copy-start.1
  63.1 8.7 %all-to-all-start.2 = ((f32[64,16,512]{2,1,0:T(8,128)}), f32[64,16,512]{2,1,0:T(8,128)S(1)}, u32[]{:S(2)}, u32[]{:S(2)}) async-start(f32[64,16,512]{2,1,0:T(8,128)} %bitcast.16), calls=%async_computation.2 | async-start | bytes 4194304 | tf_op jit(solution)/shard_map/all_to_all | solution.py:247
  71.9 0.9 collective-permute-start.3
  72.8 0.0 copy-done.1
  72.8 1.2 collective-permute-start
  74.0 0.0 copy-done.2
  74.0 0.0 collective-permute-start.4
  74.0 23.4 %collective-permute-done.3.p1 = bf16[1024,256]{1,0:T(8,128)(2,1)} collective-permute-done((bf16[1024,256]{1,0:T(8,128)(2,1)S(1)}, bf16[1024,256]{1,0:T(8,128)(2,1)}, u32[]{:S(2)}, u32[]{:S(2)}) %collective-permute-start.3) | collective-permute-done | bytes 524320 | tf_op jit(solution)/shard_map/ppermute | solution.py:261
  97.4 0.0 collective-permute-start.5
  97.4 0.5 collective-permute-start.1
  97.9 16.7 %collective-permute-done.f1 = bf16[1024,256]{1,0:T(8,128)(2,1)} collective-permute-done((bf16[1024,256]{1,0:T(8,128)(2,1)S(1)}, bf16[1024,256]{1,0:T(8,128)(2,1)}, u32[]{:S(2)}, u32[]{:S(2)}) %collective-permute-start) | collective-permute-done | bytes 524320 | tf_op jit(solution)/shard_map/ppermute | solution.py:261
  114.6 0.0 collective-permute-start.2
  114.6 5.1 %all-to-all-done.2 = f32[64,16,512]{2,1,0:T(8,128)S(1)} async-done(((f32[64,16,512]{2,1,0:T(8,128)}), f32[64,16,512]{2,1,0:T(8,128)S(1)}, u32[]{:S(2)}, u32[]{:S(2)}) %all-to-all-start.2) | async-done | bytes 2097184 | tf_op jit(solution)/shard_map/all_to_all | solution.py:247
  119.7 0.1 reduce_sum.22
  119.9 1.6 broadcast_in_dim.15
  121.4 9.5 %all-to-all-start.3 = ((f32[64,16,512]{2,1,0:T(8,128)}), f32[64,16,512]{2,1,0:T(8,128)S(1)}, u32[]{:S(2)}, u32[]{:S(2)}) async-start(f32[64,16,512]{2,1,0:T(8,128)} %broadcast_in_dim.15), calls=%async_computation.3 | async-start | bytes 4194304 | tf_op jit(solution)/shard_map/all_to_all | solution.py:247
  131.0 0.0 collective-permute-done.4.p2
  131.0 0.0 collective-permute-done.5.p3
  131.0 51.1 %factor.1 = (f32[1024,1024]{1,0:T(8,128)}, f32[8,1024]{1,0:T(8,128)}) custom-call(bf16[1024,256]{1,0:T(8,128)(2,1)} %bitcast.19, bf16[1024,256]{1,0:T(8,128)(2,1)} %collective-permute-done.3.p1, bf16[1024,256]{1,0:T(8,128)(2,1)} %collective-permute-done.4.p2, bf16[1024,256]{1,0:T(8,128)(2,1)} %collective-permute-done.5.p3), custom_call_target="tpu_custom_call" | custom-call | flops 40000000000 | bytes 8388608 | tf_op jit(solution)/shard_map/factor/pallas_call | solution.py:205
  182.1 0.0 collective-permute-done.1.f2
  182.1 0.0 collective-permute-done.2.f3
  182.1 18.0 %response.1.v_ref = f32[1024,1024]{1,0:T(8,128)} custom-call(bf16[1024,256]{1,0:T(8,128)(2,1)} %f0.1, bf16[1024,256]{1,0:T(8,128)(2,1)} %collective-permute-done.f1, bf16[1024,256]{1,0:T(8,128)(2,1)} %collective-permute-done.1.f2, bf16[1024,256]{1,0:T(8,128)(2,1)} %collective-permute-done.2.f3, bf16[1024,256]{1,0:T(8,128)(2,1)} %bitcast.20, ...), custom_call_target="tpu_custom_call" | custom-call | flops 12884901888 | bytes 8388608 | tf_op jit(solution)/shard_map/response/pallas_call | solution.py:218
  200.1 0.0 all-to-all-done.3
  200.1 0.0 copy-start
  200.1 0.7 broadcast_in_dim.6.idx_ref
  200.7 0.7 copy-done
  201.5 21.9 %tail.1 = (f32[1024,512]{1,0:T(8,128)}, f32[1024,512]{1,0:T(8,128)}) custom-call(s32[8,1024]{1,0:T(8,128)} %broadcast_in_dim.6.idx_ref, f32[1024,512]{1,0:T(8,128)} %t_ref.3, f32[1024,1024]{1,0:T(8,128)} %response.1.v_ref, f32[1024,1024]{1,0:T(8,128)} %get-tuple-element.8.w_ref, f32[1024,512]{1,0:T(8,128)} %bitcast.12), custom_call_target="tpu_custom_call" | custom-call | tf_op jit(solution)/shard_map/tail/pallas_call | solution.py:235
  (2 shorter events, 0.0 us)
Async XLA Ops:
  38.4 24.7 %all-to-all-start.1 = ((bf16[64,16,256]{2,1,0:T(8,128)(2,1)}), bf16[64,16,256]{2,1,0:T(8,128)(2,1)S(1)}, u32[]{:S(2)}, u32[]{:S(2)}) async-start(bf16[64,16,256]{2,1,0:T(8,128)(2,1)} %broadcast_in_dim.14), calls=%async_computation.1 | async-start | bytes 1048576 | tf_op jit(solution)/shard_map/all_to_all | solution.py:247
  63.1 10.9 %copy-start.2 = (bf16[64,16,256]{2,1,0:T(8,128)(2,1)}, bf16[64,16,256]{2,1,0:T(8,128)(2,1)S(1)}, u32[]{:S(2)}) copy-start(bf16[64,16,256]{2,1,0:T(8,128)(2,1)S(1)} %all-to-all-done.1) | copy-start | bytes 1572868
  63.1 9.6 %copy-start.1 = (bf16[1024,256]{1,0:T(8,128)(2,1)S(1)}, bf16[1024,256]{1,0:T(8,128)(2,1)}, u32[]{:S(2)}) copy-start(bf16[1024,256]{1,0:T(8,128)(2,1)} %f0.1) | copy-start | bytes 1572868
  63.1 56.6 %all-to-all-start.2 = ((f32[64,16,512]{2,1,0:T(8,128)}), f32[64,16,512]{2,1,0:T(8,128)S(1)}, u32[]{:S(2)}, u32[]{:S(2)}) async-start(f32[64,16,512]{2,1,0:T(8,128)} %bitcast.16), calls=%async_computation.2 | async-start | bytes 4194304 | tf_op jit(solution)/shard_map/all_to_all | solution.py:247
  71.9 25.5 %collective-permute-start.3 = (bf16[1024,256]{1,0:T(8,128)(2,1)S(1)}, bf16[1024,256]{1,0:T(8,128)(2,1)}, u32[]{:S(2)}, u32[]{:S(2)}) collective-permute-start(bf16[1024,256]{1,0:T(8,128)(2,1)S(1)} %bitcast.17), channel_id=1, source_target_pairs={{0,2},{2,0},{1,3},{3,1},{4,6},{6,4},{5,7},{7,5},{8,10},{10,8},{9,1... | collective-permute-start | bytes 1572872 | tf_op jit(solution)/shard_map/ppermute | solution.py:261
  72.8 41.9 %collective-permute-start = (bf16[1024,256]{1,0:T(8,128)(2,1)S(1)}, bf16[1024,256]{1,0:T(8,128)(2,1)}, u32[]{:S(2)}, u32[]{:S(2)}) collective-permute-start(bf16[1024,256]{1,0:T(8,128)(2,1)S(1)} %copy-done.1), channel_id=1, source_target_pairs={{0,2},{2,0},{1,3},{3,1},{4,6},{6,4},{5,7},{7,5},{8,10},{10,8},{9,1... | collective-permute-start | bytes 1572872 | tf_op jit(solution)/shard_map/ppermute | solution.py:261
  74.0 57.0 %collective-permute-start.4 = (bf16[1024,256]{1,0:T(8,128)(2,1)S(1)}, bf16[1024,256]{1,0:T(8,128)(2,1)}, u32[]{:S(2)}, u32[]{:S(2)}) collective-permute-start(bf16[1024,256]{1,0:T(8,128)(2,1)S(1)} %bitcast.18), channel_id=1, source_target_pairs={{0,1},{1,0},{2,3},{3,2},{4,5},{5,4},{6,7},{7,6},{8,9},{9,8},{10,11... | collective-permute-start | bytes 1572872 | tf_op jit(solution)/shard_map/ppermute | solution.py:262
  97.4 33.6 %collective-permute-start.5 = (bf16[1024,256]{1,0:T(8,128)(2,1)}, bf16[1024,256]{1,0:T(8,128)(2,1)}, u32[]{:S(2)}, u32[]{:S(2)}) collective-permute-start(bf16[1024,256]{1,0:T(8,128)(2,1)} %collective-permute-done.3.p1), channel_id=1, source_target_pairs={{0,1},{1,0},{2,3},{3,2},{4,5},{5,4},{6,7},{7,6},{8,9},{9,8},{10,11... | collective-permute-start | bytes 1572872 | tf_op jit(solution)/shard_map/ppermute | solution.py:262
  97.4 84.7 %collective-permute-start.1 = (bf16[1024,256]{1,0:T(8,128)(2,1)S(1)}, bf16[1024,256]{1,0:T(8,128)(2,1)}, u32[]{:S(2)}, u32[]{:S(2)}) collective-permute-start(bf16[1024,256]{1,0:T(8,128)(2,1)S(1)} %copy-done.1), channel_id=1, source_target_pairs={{0,1},{1,0},{2,3},{3,2},{4,5},{5,4},{6,7},{7,6},{8,9},{9,8},{10,11... | collective-permute-start | bytes 1572872 | tf_op jit(solution)/shard_map/ppermute | solution.py:262
  114.6 67.4 %collective-permute-start.2 = (bf16[1024,256]{1,0:T(8,128)(2,1)}, bf16[1024,256]{1,0:T(8,128)(2,1)}, u32[]{:S(2)}, u32[]{:S(2)}) collective-permute-start(bf16[1024,256]{1,0:T(8,128)(2,1)} %collective-permute-done.f1), channel_id=1, source_target_pairs={{0,1},{1,0},{2,3},{3,2},{4,5},{5,4},{6,7},{7,6},{8,9},{9,8},{10,11... | collective-permute-start | bytes 1572872 | tf_op jit(solution)/shard_map/ppermute | solution.py:262
  121.4 78.6 %all-to-all-start.3 = ((f32[64,16,512]{2,1,0:T(8,128)}), f32[64,16,512]{2,1,0:T(8,128)S(1)}, u32[]{:S(2)}, u32[]{:S(2)}) async-start(f32[64,16,512]{2,1,0:T(8,128)} %broadcast_in_dim.15), calls=%async_computation.3 | async-start | bytes 4194304 | tf_op jit(solution)/shard_map/all_to_all | solution.py:247
  200.1 1.4 copy-start

commit v2 on v1

--- a/solution.py
+++ b/solution.py
@@ -14,6 +14,8 @@
 LEAF = 128
 HI = lax.Precision.HIGHEST
 SWAP = [(0, 1), (1, 0)]
+SLOTS = 32
+CAP = 96
 
 
 def mm(a, b):
@@ -66,6 +68,21 @@
     return m
 
 
+def leaf_inverse_small(m):
+    n = m.shape[-1]
+    lane = lax.broadcasted_iota(jnp.int32, (1, 1, n), 2)
+    sub = lax.broadcasted_iota(jnp.int32, (1, n, 1), 1)
+
+    def step(j, m):
+        c = jnp.sum(jnp.where(lane == j, m, 0.0), axis=2, keepdims=True)
+        r = jnp.sum(jnp.where(sub == j, m, 0.0), axis=1, keepdims=True)
+        ip = 1.0 / jnp.sum(jnp.where(lane == j, r, 0.0), axis=2, keepdims=True)
+        r = jnp.where(lane == j, ip, r * ip)
+        return jnp.where(sub == j, r, jnp.where(lane == j, 0.0, m) - c * r)
+
+    return lax.fori_loop(0, n, step, m)
+
+
 def pick_points_kernel(idx_ref, f_ref, o_ref):
     n = f_ref.shape[0]
     sel = (idx_ref[...] == lax.broadcasted_iota(jnp.int32, (idx_ref.shape[0], n), 1)).astype(jnp.bfloat16)
@@ -93,7 +110,25 @@
     o_ref[...] = (got[:, :w] + got[:, w : 2 * w]) + got[:, 2 * w :]
 
 
-def factor_kernel(p0, p1, p2, p3, w_ref, pn_ref, a_ref, r_ref, *, width):
+def invert_blocks(a_ref, r_ref, leaf):
+    n = a_ref.shape[1]
+
+    def step(k, carry):
+        at = pl.ds(pl.multiple_of(k * LEAF, LEAF), LEAF)
+        dinv = leaf(a_ref[:, at, at])
+        for s in range(2):
+            r_ref[s] = mm(dinv[s], a_ref[s, at, :])
+            r_ref[s, :, at] = dinv[s]
+            col = a_ref[s, :, at]
+            a_ref[s, :, at] = jnp.zeros((n, LEAF), jnp.float32)
+            a_ref[s] = a_ref[s] - mm(col, r_ref[s])
+            a_ref[s, at, :] = r_ref[s]
+        return carry
+
+    lax.fori_loop(0, n // LEAF, step, 0)
+
+
+def factor_kernel(p0, p1, p2, p3, k_ref, pn_ref, a_ref, r_ref, *, width, leaf):
     points = (p0, p1, p2, p3)
     n = p0.shape[0] // 2
     gram = lambda a, b: sum(mm_nt(p[a * n : (a + 1) * n, :], p[b * n : (b + 1) * n, :]) for p in points)
@@ -108,28 +143,16 @@
         k = jnp.exp(scale * (cols[s] + rows[s] - 2.0 * g))
         a_ref[s] = k + jnp.where(eye, RIDGE, 0.0)
         pn_ref[:, s * n : (s + 1) * n] = jnp.broadcast_to(rows[s], (8, n))
-    w_ref[n:, :n] = jnp.exp(scale * (cols[1] + rows[0] - 2.0 * gram(1, 0)))
-    w_ref[:n, n:] = jnp.zeros((n, n), jnp.float32)
-
-    def step(k, carry):
-        at = pl.ds(pl.multiple_of(k * LEAF, LEAF), LEAF)
-        dinv = leaf_inverse(a_ref[:, at, at])
-        for s in range(2):
-            r_ref[s] = mm(dinv[s], a_ref[s, at, :])
-            r_ref[s, :, at] = dinv[s]
-            col = a_ref[s, :, at]
-            a_ref[s, :, at] = jnp.zeros((n, LEAF), jnp.float32)
-            a_ref[s] = a_ref[s] - mm(col, r_ref[s])
-            a_ref[s, at, :] = r_ref[s]
-        return carry
-
-    lax.fori_loop(0, n // LEAF, step, 0)
-    w_ref[:n, :n] = a_ref[0]
-    w_ref[n:, n:] = a_ref[1]
-    w_ref[n:, :n] = -mm(a_ref[1], mm(w_ref[n:, :n], a_ref[0]))
-
-
-def response_kernel(f0, f1, f2, f3, p0, p1, p2, p3, pn_ref, w_ref, v_ref, *, width):
+    k_ref[...] = jnp.exp(scale * (cols[1] + rows[0] - 2.0 * gram(1, 0)))
+    invert_blocks(a_ref, r_ref, leaf)
+
+
+def split2(x):
+    hi = x.astype(jnp.bfloat16)
+    return hi, (x - hi.astype(jnp.float32)).astype(jnp.bfloat16)
+
+
+def slab_kernel(f0, f1, f2, f3, p0, p1, p2, p3, pn_ref, s_ref, *, width):
     g = None
     sq = None
     for f, p in ((f0, p0), (f1, p1), (f2, p2), (f3, p3)):
@@ -139,28 +162,175 @@
         xf = x.astype(jnp.float32)
         xs = xf * xf
         sq = xs if sq is None else sq + xs
-    n = w_ref.shape[0] // 2
+    m = p0.shape[0]
     slab = jnp.exp(-(2.0 / width) * (jnp.sum(sq, axis=1, keepdims=True) + pn_ref[0:1, :] - 2.0 * g))
-    v_ref[:, :n] = mm(slab, w_ref[:, :n])
-    v_ref[:, n:] = mm(slab[:, n:], w_ref[n:, n:])
-
-
-def tail_kernel(idx_ref, t_ref, v_ref, w_ref, tp_ref, c_ref, r_ref, parts):
+    s_ref[:, :m], s_ref[:, m:] = split2(slab)
+
+
+def solve_into(tp, x_ref, k_ref, delta, parts):
+    n = x_ref.shape[1]
+    w = delta.shape[1]
+    first = mm(x_ref[0], tp[0:n, :])
+    second = mm(x_ref[1], tp[n : 2 * n, :] - mm(k_ref[...], first))
+    delta[0:n, :] = first
+    delta[n : 2 * n, :] = second
+    parts[0:n, :w], parts[0:n, w:] = split2(first)
+    parts[n : 2 * n, :w], parts[n : 2 * n, w:] = split2(second)
+
+
+def fitted(s_ref, parts):
+    m, w = parts.shape[0], parts.shape[1] // 2
+    both = jnp.dot(s_ref[:, :m], parts[...], preferred_element_type=jnp.float32)
+    low = jnp.dot(s_ref[:, m:], parts[:, :w], preferred_element_type=jnp.float32)
+    return both[:, :w] + (both[:, w:] + low)
+
+
+def lay_out(counts, b_ref, dense):
+    groups = counts.shape[0] // 2
+    lanes = dense.shape[1]
+    row = lax.broadcasted_iota(jnp.int32, (CAP + 8, lanes), 0)
+    for s in range(2):
+        at = jnp.int32(s * ((dense.shape[0] - CAP - 8) // 2))
+        for g in range(groups):
+            src = (2 * g + s) * CAP
+            shift = at & 7
+            window = pl.ds(pl.multiple_of(at - shift, 8), CAP + 8)
+            x = jnp.concatenate([b_ref[src : src + CAP, :], b_ref[src : src + 8, :]], axis=0)
+            dense[window, :] = jnp.where(row >= shift, pltpu.roll(x, shift, 0), dense[window, :])
+            at = at + counts[2 * g + s]
+
+
+def dense_points_kernel(counts, b_ref, o_ref, wide, dense):
+    wide[...] = b_ref[...].astype(jnp.float32)
+
+    lay_out(counts, wide, dense)
+    o_ref[...] = dense[0 : o_ref.shape[0], :].astype(jnp.bfloat16)
+
+
+def tail_kernel(counts, own_row, own_pos, t_ref, s_ref, x_ref, k_ref, b_ref, c_ref, r_ref, tp, delta, parts):
+    rows = t_ref.shape[0]
+    base = pl.program_id(0) * rows
+
+    @pl.when(pl.program_id(0) == 0)
+    def _():
+        lay_out(counts, b_ref, tp)
+        solve_into(tp, x_ref, k_ref, delta, parts)
+
+    c_ref[...] = jnp.zeros(c_ref.shape, jnp.float32)
+    r_ref[...] = t_ref[...] - fitted(s_ref, parts)
+    for q in range(SLOTS):
+        row = own_row[q] - base
+
+        @pl.when((row >= 0) & (row < rows))
+        def _():
+            got = delta[pl.ds(own_pos[q], 1), :]
+            c_ref[pl.ds(row, 1), :] = got
+            r_ref[pl.ds(row, 1), :] = r_ref[pl.ds(row, 1), :] - RIDGE * got
+
+
+def slow_tail_kernel(idx_ref, t_ref, s_ref, x_ref, k_ref, tp_ref, c_ref, r_ref, delta, parts, exact):
     n, w = tp_ref.shape
     rows = t_ref.shape[0]
 
     @pl.when(pl.program_id(0) == 0)
     def _():
-        delta = mm(w_ref[...], tp_ref[...])
-        for i, part in enumerate(split3(delta)):
-            parts[:, i * w : (i + 1) * w] = part
+        solve_into(tp_ref, x_ref, k_ref, delta, parts)
+        for i, part in enumerate(split3(delta[...])):
+            exact[:, i * w : (i + 1) * w] = part
 
     row = lax.broadcasted_iota(jnp.int32, (rows, n), 0) + pl.program_id(0) * rows
     sel = (idx_ref[0:1, :] == row).astype(jnp.bfloat16)
-    got = jnp.dot(sel, parts[...], preferred_element_type=jnp.float32)
+    got = jnp.dot(sel, exact[...], preferred_element_type=jnp.float32)
     coefs = (got[:, :w] + got[:, w : 2 * w]) + got[:, 2 * w :]
     c_ref[...] = coefs
-    r_ref[...] = t_ref[...] - mm(v_ref[...], tp_ref[...]) - RIDGE * coefs
+    r_ref[...] = t_ref[...] - fitted(s_ref, parts) - RIDGE * coefs
+
+
+def prefix(mask, tri):
+    n, total = mask.shape[0], jnp.zeros((mask.shape[0], 1), jnp.float32)
+    out = []
+    for b in range(mask.shape[1] // 128):
+        part = mask[:, b * 128 : (b + 1) * 128]
+        out.append(jnp.dot(part.astype(jnp.bfloat16), tri, preferred_element_type=jnp.float32) + total)
+        total = total + jnp.sum(part, axis=1, keepdims=True)
+    return jnp.concatenate(out, axis=1), total
+
+
+def plan_kernel(me, b_ref, f_ref, own_ref, list_ref, count_ref, p_ref, *, shift, far, mid, near):
+    xh, z, y = me[0], me[1], me[2]
+    lanes = b_ref.shape[1]
+    idx = jnp.concatenate([b_ref[0:1, :], b_ref[1:2, :]], axis=1)
+    m = idx.shape[1]
+    one = lambda c: jnp.where(c, 1.0, 0.0)
+    owner = lax.shift_right_logical(idx, shift)
+    row = (idx & ((1 << shift) - 1)).astype(jnp.float32)
+    hi = owner // (mid * near)
+    oz = (owner // near) % mid
+    oy = owner % near
+    group = hi * near + oy
+    my_group = xh * near + y
+    step = (lax.broadcasted_iota(jnp.int32, (1, m), 1) >= lanes).astype(jnp.int32)
+    tri = one(
+        lax.broadcasted_iota(jnp.int32, (128, 128), 0) < lax.broadcasted_iota(jnp.int32, (128, 128), 1)
+    ).astype(jnp.bfloat16)
+    mine = group == my_group
+    masks = one((oz == lax.broadcasted_iota(jnp.int32, (mid, m), 0)) & mine)
+    rank_all, _ = prefix(masks, tri)
+    rank = jnp.sum(rank_all * masks, axis=0, keepdims=True)
+    cls = one((step == lax.broadcasted_iota(jnp.int32, (8, m), 0)) & mine)
+    crank_all, _ = prefix(cls, tri)
+    crank = jnp.sum(crank_all * cls, axis=0, keepdims=True)
+    own = mine & (oz == z)
+    slot = lax.broadcasted_iota(jnp.int32, (SLOTS, m), 0).astype(jnp.float32)
+    hit = own & (slot == rank)
+    before = one(group < my_group)
+    early = (step == 0).astype(jnp.float32)
+    off0 = jnp.sum(before * early, axis=1, keepdims=True)
+    off1 = jnp.sum(before * (1.0 - early), axis=1, keepdims=True)
+    pos = jnp.where(step == 0, off0, off1 + float(lanes)) + crank
+    take = lambda hits, v: jnp.sum(jnp.where(hits, v + 1.0, 0.0), axis=1, keepdims=True) - 1.0
+    own_row = take(hit, row)
+    column = lax.broadcasted_iota(jnp.int32, (SLOTS, 128), 1)
+    both = jnp.where(column == 0, own_row, take(hit, pos))
+    own_ref[...] = both.astype(jnp.int32)
+    v = oz.astype(jnp.float32) * float(SLOTS) + rank
+    for s in range(2):
+        half = slice(s * lanes, (s + 1) * lanes)
+        u = lax.broadcasted_iota(jnp.int32, (CAP, lanes), 0).astype(jnp.float32)
+        got = take(mine[:, half] & (u == crank[:, half]), v[:, half])
+        list_ref[s * CAP : (s + 1) * CAP, :] = jnp.broadcast_to(got, (CAP, 128)).astype(jnp.int32)
+    code = 2 * group + step
+    classes = 2 * far * near
+    count = jnp.sum(one(code == lax.broadcasted_iota(jnp.int32, (classes, m), 0)), axis=1, keepdims=True)
+    owners = far * mid * near
+    used = jnp.sum(one(owner == lax.broadcasted_iota(jnp.int32, (owners, m), 0)), axis=1, keepdims=True)
+    over = one(jnp.max(used, axis=0, keepdims=True) > float(SLOTS)) + one(
+        jnp.max(count, axis=0, keepdims=True) > float(CAP)
+    )
+    count_ref[0:classes, :] = jnp.broadcast_to(count, (classes, 128)).astype(jnp.int32)
+    count_ref[classes:, :] = jnp.broadcast_to(over, (8, 128)).astype(jnp.int32)
+    n = f_ref.shape[0]
+    at = lax.broadcasted_iota(jnp.int32, (SLOTS, n), 1).astype(jnp.float32)
+    sel = one(own_row == at).astype(jnp.bfloat16)
+    p_ref[...] = jnp.dot(sel, f_ref[...], preferred_element_type=jnp.float32).astype(jnp.bfloat16)
+
+
+def own_targets_kernel(own_row, t_ref, o_ref):
+    for q in range(SLOTS):
+        row = own_row[q]
+        got = t_ref[pl.ds(jnp.maximum(row, 0), 1), :]
+        o_ref[q : q + 1, :] = jnp.where(row >= 0, got, 0.0)
+
+
+def pack_kernel(list_ref, b_ref, o_ref):
+    m, n = list_ref.shape[0], b_ref.shape[0]
+    sel = jnp.where(list_ref[:, 0:1] == lax.broadcasted_iota(jnp.int32, (m, n), 1), 1.0, 0.0).astype(jnp.bfloat16)
+    b = b_ref[...]
+    if b.dtype == jnp.bfloat16:
+        o_ref[...] = jnp.dot(sel, b, preferred_element_type=jnp.float32).astype(jnp.bfloat16)
+    else:
+        hi, mid, low = (jnp.dot(sel, part, preferred_element_type=jnp.float32) for part in split3(b))
+        o_ref[...] = (hi + mid) + low
 
 
 def full(shape):
@@ -199,48 +369,137 @@
     )(idx_col, t)
 
 
-def factor(points, width):
+def factor(points, width, leaf):
     m = points[0].shape[0]
     n = m // 2
     return pl.pallas_call(
-        functools.partial(factor_kernel, width=width),
-        out_shape=(jax.ShapeDtypeStruct((m, m), jnp.float32), jax.ShapeDtypeStruct((8, m), jnp.float32)),
-        scratch_shapes=[pltpu.VMEM((2, n, n), jnp.float32), pltpu.VMEM((2, LEAF, n), jnp.float32)],
+        functools.partial(factor_kernel, width=width, leaf=leaf),
+        out_shape=(
+            jax.ShapeDtypeStruct((n, n), jnp.float32),
+            jax.ShapeDtypeStruct((8, m), jnp.float32),
+            jax.ShapeDtypeStruct((2, n, n), jnp.float32),
+        ),
+        in_specs=[pl.BlockSpec(memory_space=pltpu.VMEM)] * 4,
+        out_specs=(pl.BlockSpec(memory_space=pltpu.VMEM),) * 3,
+        scratch_shapes=[pltpu.VMEM((2, LEAF, n), jnp.float32)],
         name="factor",
         cost_estimate=pl.CostEstimate(flops=40 * 10**9, transcendentals=0, bytes_accessed=8 * m * m),
     )(*points)
 
 
-def response(own, points, pn, w, width):
+def slab_of(own, points, pn, width):
     n = own[0].shape[0]
-    m = w.shape[0]
+    m = points[0].shape[0]
     bm = 256
     return pl.pallas_call(
-        functools.partial(response_kernel, width=width),
+        functools.partial(slab_kernel, width=width),
         grid=(n // bm,),
-        in_specs=[tile(bm, x.shape[1]) for x in own]
-        + [full(x.shape) for x in points]
-        + [full(pn.shape), full(w.shape)],
-        out_specs=tile(bm, m),
-        out_shape=jax.ShapeDtypeStruct((n, m), jnp.float32),
-        name="response",
-        cost_estimate=pl.CostEstimate(flops=12 * n * m * m, transcendentals=0, bytes_accessed=8 * m * m),
-    )(*own, *points, pn, w)
-
-
-def tail(idx_row, t, v, w, tp):
+        in_specs=[tile(bm, x.shape[1]) for x in own] + [full(x.shape) for x in points] + [full(pn.shape)],
+        out_specs=tile(bm, 2 * m),
+        out_shape=jax.ShapeDtypeStruct((n, 2 * m), jnp.bfloat16),
+        name="slab",
+        cost_estimate=pl.CostEstimate(flops=2 * n * m * width, transcendentals=0, bytes_accessed=8 * n * m),
+    )(*own, *points, pn)
+
+
+SMEM = pl.BlockSpec(memory_space=pltpu.SMEM)
+
+
+def tail(counts, own_row, own_pos, t, slab, x, k, buffer):
     n, width = t.shape
-    m = w.shape[0]
+    m = 2 * k.shape[0]
     bm = 256
     return pl.pallas_call(
         tail_kernel,
         grid=(n // bm,),
-        in_specs=[full(idx_row.shape), tile(bm, width), tile(bm, m), full(w.shape), full(tp.shape)],
+        in_specs=[SMEM, SMEM, SMEM, tile(bm, width), tile(bm, 2 * m), full(x.shape), full(k.shape), full(buffer.shape)],
         out_specs=(tile(bm, width), tile(bm, width)),
         out_shape=(jax.ShapeDtypeStruct(t.shape, jnp.float32),) * 2,
-        scratch_shapes=[pltpu.VMEM((m, 3 * width), jnp.bfloat16)],
+        scratch_shapes=[
+            pltpu.VMEM((m + CAP + 8, width), jnp.float32),
+            pltpu.VMEM((m, width), jnp.float32),
+            pltpu.VMEM((m, 2 * width), jnp.bfloat16),
+        ],
         name="tail",
-    )(idx_row, t, v, w, tp)
+    )(counts, own_row, own_pos, t, slab, x, k, buffer)
+
+
+def slow_tail(idx_row, t, slab, x, k, tp):
+    n, width = t.shape
+    m = tp.shape[0]
+    bm = 256
+    return pl.pallas_call(
+        slow_tail_kernel,
+        grid=(n // bm,),
+        in_specs=[full(idx_row.shape), tile(bm, width), tile(bm, 2 * m), full(x.shape), full(k.shape), full(tp.shape)],
+        out_specs=(tile(bm, width), tile(bm, width)),
+        out_shape=(jax.ShapeDtypeStruct(t.shape, jnp.float32),) * 2,
+        scratch_shapes=[
+            pltpu.VMEM((m, width), jnp.float32),
+            pltpu.VMEM((m, 2 * width), jnp.bfloat16),
+            pltpu.VMEM((m, 3 * width), jnp.bfloat16),
+        ],
+        name="slow_tail",
+    )(idx_row, t, slab, x, k, tp)
+
+
+def plan(me, block_index, f, sizes):
+    far, mid, near = sizes
+    n, w = f.shape
+    vmem = pl.BlockSpec(memory_space=pltpu.VMEM)
+    i32 = jnp.int32
+    return pl.pallas_call(
+        functools.partial(plan_kernel, shift=n.bit_length() - 1, far=far, mid=mid, near=near),
+        in_specs=[SMEM, vmem, vmem],
+        out_specs=(vmem,) * 4,
+        out_shape=(
+            jax.ShapeDtypeStruct((SLOTS, 128), i32),
+            jax.ShapeDtypeStruct((2 * CAP, 128), i32),
+            jax.ShapeDtypeStruct((2 * far * near + 8, 128), i32),
+            jax.ShapeDtypeStruct((SLOTS, w), f.dtype),
+        ),
+        name="plan",
+    )(me, block_index, f)
+
+
+def own_targets(own_row, t):
+    return pl.pallas_call(
+        own_targets_kernel,
+        in_specs=[SMEM, pl.BlockSpec(memory_space=pltpu.VMEM)],
+        out_specs=pl.BlockSpec(memory_space=pltpu.VMEM),
+        out_shape=jax.ShapeDtypeStruct((SLOTS, t.shape[1]), t.dtype),
+        name="own_targets",
+    )(own_row, t)
+
+
+def pack(where, buffer):
+    vmem = pl.BlockSpec(memory_space=pltpu.VMEM)
+    return pl.pallas_call(
+        pack_kernel,
+        in_specs=[vmem, vmem],
+        out_specs=vmem,
+        out_shape=jax.ShapeDtypeStruct((where.shape[0], buffer.shape[1]), buffer.dtype),
+        name="pack",
+    )(where, buffer)
+
+
+def dense_points(counts, buffer, m):
+    w = buffer.shape[1]
+    vmem = pl.BlockSpec(memory_space=pltpu.VMEM)
+    return pl.pallas_call(
+        dense_points_kernel,
+        in_specs=[SMEM, vmem],
+        out_specs=vmem,
+        out_shape=jax.ShapeDtypeStruct((m, w), buffer.dtype),
+        scratch_shapes=[pltpu.VMEM(buffer.shape, jnp.float32), pltpu.VMEM((m + CAP + 8, w), jnp.float32)],
+        name="dense_points",
+    )(counts, buffer)
+
+
+def spread(x, axes):
+    parts = jnp.broadcast_to(x, (lax.axis_size(axes), *x.shape))
+    parts = lax.all_to_all(parts, axes, split_axis=0, concat_axis=0, tiled=True)
+    return parts.reshape(-1, x.shape[1])
 
 
 def exchange(parts):
@@ -262,23 +521,43 @@
     return (x, other, lax.ppermute(x, "core", SWAP), lax.ppermute(other, "core", SWAP))
 
 
-def shards(features, targets, block_index):
+def slow(features, targets, block_index):
     rows_here = features.shape[0]
     count = lax.axis_size(ROWS)
     width = features.shape[1] * lax.axis_size(COLS)
-    start = lax.axis_index(ROWS) * rows_here
-    idx = block_index.reshape(-1) - start
+    idx = block_index.reshape(-1) - lax.axis_index(ROWS) * rows_here
     idx_col = idx[:, None]
     idx_row = jnp.broadcast_to(idx[None, :], (8, idx.shape[0]))
     own = over_cols(features)
-    p = gathered(scattered_sum(pick_points(idx_col, features), count), count)
-    t = pick_targets(idx_col, targets)
-    t, p = lax.optimization_barrier((t, p))
+    points = over_cols(gathered(scattered_sum(pick_points(idx_col, features), count), count))
+    tp = gathered(scattered_sum(pick_targets(idx_col, targets), count), count)
+    k, pn, x = factor(points, width, leaf_inverse_small)
+    return tuple(slow_tail(idx_row, targets, slab_of(own, points, pn, width), x, k, tp))
+
+
+def shards(features, targets, block_index):
+    width = features.shape[1] * lax.axis_size(COLS)
+    sizes = tuple(lax.axis_size(a) for a in ROWS)
+    me = jnp.stack([lax.axis_index(a) for a in ROWS]).astype(jnp.int32)
+    across = (ROWS[0], ROWS[2])
+    own_list, where, counts, p = plan(me, block_index, features, sizes)
+    own_row, own_pos = own_list[:, 0], own_list[:, 1]
+    classes = counts.shape[0] - 8
+    overflow = counts[classes, 0] > 0
+    counts = counts[:classes, 0]
+    own = over_cols(features)
+    p = pack(where, spread(p, ROWS[1]))
+    p = dense_points(counts, spread(p, across), block_index.size)
+    t, p = lax.optimization_barrier((own_targets(own_row, targets), p))
     points = over_cols(p)
-    tp = gathered(scattered_sum(t, count), count)
-    w, pn = factor(points, width)
-    v = response(own, points, pn, w, width)
-    return tail(idx_row, targets, v, w, tp)
+    t = spread(pack(where, spread(t, ROWS[1])), across)
+    k, pn, x = factor(points, width, leaf_inverse)
+    slab = slab_of(own, points, pn, width)
+    return lax.cond(
+        overflow,
+        lambda: slow(features, targets, block_index),
+        lambda: tuple(tail(counts, own_row, own_pos, targets, slab, x, k, t)),
+    )
 
 
 def solution(mesh):

time: 226 us -> 155 us (0.69)
  waiting for transfers between devices: 53.8 us -> 24.4 us
  Pallas kernels: 102 us -> 79.9 us
  blocking collectives: 31 us -> 17.5 us
  starting transfers between devices: 29.7 us -> 19 us
  local copies, waits for them, and re-layouts: 4.82 us -> 10.4 us
    ppermute x2, waiting for transfers between devices: 40.1 us -> 16.1 us  [over_cols(): other = lax.ppermute(x, 'xlo', SWAP)]
    pallas_call x5 -> x8, Pallas kernels: 102 us -> 79.9 us  [the longest x1 46.6 us: factor(): pl.pallas_call(functools.partial(factor_kernel, width=width, leaf=leaf),...]
    all_to_all x1, blocking collectives: 31 us -> 17.5 us  [spread(): parts = lax.all_to_all(parts, axes, split_axis=0, concat_axis=0, tiled=True)]
    all_to_all x3, starting transfers between devices: 27.1 us -> 16.4 us  [spread(): parts = lax.all_to_all(parts, axes, split_axis=0, concat_axis=0, tiled=True)]
    all_to_all x3, waiting for transfers between devices: 13.6 us -> 8.3 us  [spread(): parts = lax.all_to_all(parts, axes, split_axis=0, concat_axis=0, tiled=True)]
    broadcast_in_dim x3 -> x4, local copies, waits for them, and re-layouts: 3.06 us -> 7.31 us  [spread(): parts = jnp.broadcast_to(x, (lax.axis_size(axes), *x.shape))]
  transfers between devices with their start and end apart: 9 -> 9, of which waited for: 4 -> 3; matrix products, arithmetic and copies ran while one was open for 1% -> 4% of each run, Pallas kernels for 34% -> 37%
where the time goes in v2:
time: 155 us; the launch traced here: 153 us
  Pallas kernels  79.9 us (52%)
  waiting for transfers between devices  24.4 us (16%)
  starting transfers between devices  19 us (12%)
  blocking collectives  17.5 us (11%)
  local copies, waits for them, and re-layouts  10.4 us (7%)
    pallas_call x1, Pallas kernels, factor(): pl.pallas_call(functools.partial(factor_kernel, width=width, leaf=leaf),...  46.6 us
    all_to_all x1, blocking collectives, spread(): parts = lax.all_to_all(parts, axes, split_axis=0, concat_axis=0, tiled=True)  17.5 us
    all_to_all x3, starting transfers between devices, spread(): parts = lax.all_to_all(parts, axes, split_axis=0, concat_axis=0, tiled=True)  16.4 us
    pallas_call x1, Pallas kernels, tail(): pl.pallas_call(tail_kernel, grid=(n // bm,), in_specs=[SMEM, SMEM, SMEM,...  16.2 us
    ppermute x2, waiting for transfers between devices, over_cols(): other = lax.ppermute(x, 'xlo', SWAP)  16.1 us
    all_to_all x3, waiting for transfers between devices, spread(): parts = lax.all_to_all(parts, axes, split_axis=0, concat_axis=0, tiled=True)  8.3 us
    broadcast_in_dim x4, local copies, waits for them, and re-layouts, spread(): parts = jnp.broadcast_to(x, (lax.axis_size(axes), *x.shape))  7.31 us
    pallas_call x1, Pallas kernels, slab_of(): pl.pallas_call(functools.partial(slab_kernel, width=width), grid=(n // bm...  7.04 us
  transfers between devices with their start and end apart: 9, of which 3 were waited for; matrix products, arithmetic and copies ran while one was open for 4% of the time, Pallas kernels for 37%

profile of v2, /device:TPU:6, one launch (start us, length us, event | category | flops | bytes accessed | tf_op | source)
XLA Modules:
  0.0 153.3 jit_solution(10174304692390477153)
XLA Ops:
  0.6 0.0 copy-start
  0.6 0.6 pad_add_fusion.me
  1.2 2.2 %plan.1 = (s32[32,128]{1,0:T(8,128)S(1)}, s32[192,128]{1,0:T(8,128)}, s32[24,128]{1,0:T(8,128)}, bf16[32,256]{1,0:T(8,128)(2,1)}) custom-call(s32[3]{0:T(128)} %pad_add_fusion.me, s32[2,512]{1,0:T(2,128)} %b_ref.1, bf16[1024,256]{1,0:T(8,128)(2,1)} %f0.1), custom_call_target="tpu_custom_call" | custom-call | tf_op jit(solution)/shard_map/plan/pallas_call | solution.py:451
  3.4 0.7 broadcast_in_dim.25
  4.2 17.5 %all_to_all.37 = bf16[8,32,256]{2,1,0:T(8,128)(2,1)} all-to-all(bf16[8,32,256]{2,1,0:T(8,128)(2,1)S(1)} %broadcast_in_dim.25), channel_id=1, replica_groups=mesh['r0'=2,'r1'=8,'r2'=4,'xlo'=2,'core'=2] {'r1'}, dimensions={0} | all-to-all | bytes 262144 | tf_op jit(solution)/shard_map/all_to_all | solution.py:501
  21.6 1.8 %pack.2 = bf16[192,256]{1,0:T(8,128)(2,1)} custom-call(s32[192,128]{1,0:T(8,128)} %get-tuple-element.52.list_ref, bf16[256,256]{1,0:T(8,128)(2,1)} %bitcast.32), custom_call_target="tpu_custom_call" | custom-call | tf_op jit(solution)/shard_map/pack/pallas_call | solution.py:477
  23.4 1.8 %broadcast_in_dim.26 = bf16[8,192,256]{2,1,0:T(8,128)(2,1)} broadcast(bf16[192,256]{1,0:T(8,128)(2,1)} %pack.2), dimensions={1,2} | broadcast | bytes 884736 | tf_op jit(solution)/shard_map/broadcast_in_dim | solution.py:500
  25.3 0.0 copy-start.6
  25.3 7.6 %all-to-all-start.5 = ((bf16[8,192,256]{2,1,0:T(8,128)(2,1)}), bf16[8,192,256]{2,1,0:T(8,128)(2,1)S(1)}, u32[]{:S(2)}, u32[]{:S(2)}) async-start(bf16[8,192,256]{2,1,0:T(8,128)(2,1)} %broadcast_in_dim.26), calls=%async_computation.5 | async-start | bytes 1572864 | tf_op jit(solution)/shard_map/all_to_all | solution.py:501
  32.8 0.1 slice_reduce_fusion.own_row
  32.9 0.0 copy-done
  32.9 0.0 copy-start.1
  33.0 1.3 own_targets.1
  34.2 0.0 copy-done.6
  34.2 0.1 slice_reduce_fusion.1.counts
  34.3 8.3 %all-to-all-done.5 = bf16[8,192,256]{2,1,0:T(8,128)(2,1)S(1)} async-done(((bf16[8,192,256]{2,1,0:T(8,128)(2,1)}), bf16[8,192,256]{2,1,0:T(8,128)(2,1)S(1)}, u32[]{:S(2)}, u32[]{:S(2)}) %all-to-all-start.5) | async-done | bytes 786464 | tf_op jit(solution)/shard_map/all_to_all | solution.py:501
  42.6 0.9 copy-done.2
  43.5 2.5 %dense_points.1.p0 = bf16[1024,256]{1,0:T(8,128)(2,1)} custom-call(s32[16]{0:T(128)S(1)} %slice_reduce_fusion.1.counts, bf16[1536,256]{1,0:T(8,128)(2,1)} %bitcast.22), custom_call_target="tpu_custom_call" | custom-call | tf_op jit(solution)/shard_map/dense_points/pallas_call | solution.py:489
  46.0 0.8 collective-permute-start.9
  46.8 1.7 %broadcast_in_dim.27 = f32[8,32,512]{2,1,0:T(8,128)} broadcast(f32[32,512]{1,0:T(8,128)} %own_targets.1), dimensions={1,2} | broadcast | bytes 589824 | tf_op jit(solution)/shard_map/broadcast_in_dim | solution.py:500
  48.5 3.5 %all-to-all-start.6 = ((f32[8,32,512]{2,1,0:T(8,128)}), f32[8,32,512]{2,1,0:T(8,128)S(1)}, u32[]{:S(2)}, u32[]{:S(2)}) async-start(f32[8,32,512]{2,1,0:T(8,128)} %broadcast_in_dim.27), calls=%async_computation.6 | async-start | bytes 1048576 | tf_op jit(solution)/shard_map/all_to_all | solution.py:501
  52.0 0.0 copy-done.1
  52.0 1.3 collective-permute-start.6
  53.3 0.0 collective-permute-start.10
  53.3 7.8 %collective-permute-done.9.p1 = bf16[1024,256]{1,0:T(8,128)(2,1)} collective-permute-done((bf16[1024,256]{1,0:T(8,128)(2,1)}, bf16[1024,256]{1,0:T(8,128)(2,1)}, u32[]{:S(2)}, u32[]{:S(2)}) %collective-permute-start.9) | collective-permute-done | bytes 524320 | tf_op jit(solution)/shard_map/ppermute | solution.py:520
  61.1 0.0 collective-permute-start.11
  61.1 0.5 collective-permute-start.7
  61.6 0.6 slice.13
  62.8 8.3 %collective-permute-done.6.f1 = bf16[1024,256]{1,0:T(8,128)(2,1)} collective-permute-done((bf16[1024,256]{1,0:T(8,128)(2,1)S(1)}, bf16[1024,256]{1,0:T(8,128)(2,1)}, u32[]{:S(2)}, u32[]{:S(2)}) %collective-permute-start.6) | collective-permute-done | bytes 524320 | tf_op jit(solution)/shard_map/ppermute | solution.py:520
  71.1 0.0 collective-permute-start.8
  71.1 0.0 all-to-all-done.6
  71.1 0.8 copy-done.4
  71.9 2.2 %pack.3 = f32[192,512]{1,0:T(8,128)} custom-call(s32[192,128]{1,0:T(8,128)} %get-tuple-element.52.list_ref, f32[256,512]{1,0:T(8,128)} %bitcast.31), custom_call_target="tpu_custom_call" | custom-call | tf_op jit(solution)/shard_map/pack/pallas_call | solution.py:477
  74.1 3.1 %broadcast_in_dim.28 = f32[8,192,512]{2,1,0:T(8,128)} broadcast(f32[192,512]{1,0:T(8,128)} %pack.3), dimensions={1,2} | broadcast | bytes 3538944 | tf_op jit(solution)/shard_map/broadcast_in_dim | solution.py:500
  77.2 5.3 %all-to-all-start.7 = ((f32[8,192,512]{2,1,0:T(8,128)}), f32[8,192,512]{2,1,0:T(8,128)}, u32[]{:S(2)}, u32[]{:S(2)}) async-start(f32[8,192,512]{2,1,0:T(8,128)} %broadcast_in_dim.28), calls=%async_computation.7 | async-start | bytes 6291456 | tf_op jit(solution)/shard_map/all_to_all | solution.py:501
  82.5 0.0 collective-permute-done.10.p2
  82.5 0.0 collective-permute-done.11.p3
  82.5 46.6 %factor.3 = (f32[512,512]{1,0:T(8,128)}, f32[8,1024]{1,0:T(8,128)}, f32[2,512,512]{2,1,0:T(8,128)}) custom-call(bf16[1024,256]{1,0:T(8,128)(2,1)} %dense_points.1.p0, bf16[1024,256]{1,0:T(8,128)(2,1)} %collective-permute-done.9.p1, bf16[1024,256]{1,0:T(8,128)(2,1)} %collective-permute-done.10.p2, bf16[1024,256]{1,0:T(8,128)(2,1)} %collective-permute-done.11.p3), custom_call_target="tpu_custom_call" | custom-call | flops 40000000000 | bytes 8388608 | tf_op jit(solution)/shard_map/factor/pallas_call | solution.py:375
  129.1 0.0 collective-permute-done.7.f2
  129.1 0.0 collective-permute-done.8.f3
  129.1 0.0 copy-start.5
  129.1 7.0 %slab.3 = bf16[1024,2048]{1,0:T(8,128)(2,1)} custom-call(bf16[1024,256]{1,0:T(8,128)(2,1)S(1)} %copy-done.1, bf16[1024,256]{1,0:T(8,128)(2,1)} %collective-permute-done.6.f1, bf16[1024,256]{1,0:T(8,128)(2,1)} %collective-permute-done.7.f2, bf16[1024,256]{1,0:T(8,128)(2,1)} %collective-permute-done.8.f3, bf16[1024,256]{1,0:T(8,128)(2,1)} %dense_points.1.p0, ...), custom_call_target="tpu_custom_call" | custom-call | flops 2147483648 | bytes 8388608 | tf_op jit(solution)/shard_map/slab/pallas_call | solution.py:394
  136.2 0.0 all-to-all-done.7
  136.2 0.0 copy-done.5
  136.2 17.1 %conditional.1 = ((f32[1024,512]{1,0:T(8,128)}, f32[1024,512]{1,0:T(8,128)})) conditional(s32[]{:T(128)} %bitcast.9, (s32[32,128]{1,0:T(8,128)S(1)}, f32[8,192,512]{2,1,0:T(8,128)}, s32[16]{0:T(128)S(1)}, s32[32]{0:T(128)S(1)}, f32[1024,512]{1,0:T(8,128)S(1)}, /*index=5*/bf16[1024,2048]{1,0:T(8,128)(2,1)}, f32[2,512,512]{2,1,0:T(8,128)}, ...), branch_computations={%region_0.0_spmd, %region_1.0_spmd} | conditional | flops 45369483264 | bytes 56255004 | solution.py:556
  136.4 0.1 copy.12
  136.5 0.6 slice_bitcast_fusion.own_pos
  137.1 16.2 %tail.1 = (f32[1024,512]{1,0:T(8,128)}, f32[1024,512]{1,0:T(8,128)}) custom-call(s32[16]{0:T(128)S(1)} %get-tuple-element.25.counts, s32[32]{0:T(128)S(1)} %get-tuple-element.26.own_row, s32[32]{0:T(128)} %slice_bitcast_fusion.own_pos, f32[1024,512]{1,0:T(8,128)S(1)} %get-tuple-element.28.t_ref, bf16[1024,2048]{1,0:T(8,128)(2,1)} %get-tuple-element.29.s_ref, ...), custom_call_target="tpu_custom_call" | custom-call | tf_op jit(solution)/shard_map/cond/branch_0_fun/tail/pallas_call | solution.py:412
  (2 shorter events, 0.0 us)
Async XLA Ops:
  0.6 32.3 %copy-start = (f32[1024,512]{1,0:T(8,128)S(1)}, f32[1024,512]{1,0:T(8,128)}, u32[]{:S(2)}) copy-start(f32[1024,512]{1,0:T(8,128)} %t_ref.1) | copy-start | bytes 6291460
  25.3 9.0 %copy-start.6 = (s32[24,128]{1,0:T(8,128)S(1)}, s32[24,128]{1,0:T(8,128)}, u32[]{:S(2)}) copy-start(s32[24,128]{1,0:T(8,128)} %get-tuple-element.50) | copy-start | bytes 36868
  25.3 17.4 %all-to-all-start.5 = ((bf16[8,192,256]{2,1,0:T(8,128)(2,1)}), bf16[8,192,256]{2,1,0:T(8,128)(2,1)S(1)}, u32[]{:S(2)}, u32[]{:S(2)}) async-start(bf16[8,192,256]{2,1,0:T(8,128)(2,1)} %broadcast_in_dim.26), calls=%async_computation.5 | async-start | bytes 1572864 | tf_op jit(solution)/shard_map/all_to_all | solution.py:501
  32.9 19.1 %copy-start.1 = (bf16[1024,256]{1,0:T(8,128)(2,1)S(1)}, bf16[1024,256]{1,0:T(8,128)(2,1)}, u32[]{:S(2)}) copy-start(bf16[1024,256]{1,0:T(8,128)(2,1)} %f0.1) | copy-start | bytes 1572868
  42.6 0.9 copy-start.2
  46.0 15.1 %collective-permute-start.9 = (bf16[1024,256]{1,0:T(8,128)(2,1)}, bf16[1024,256]{1,0:T(8,128)(2,1)}, u32[]{:S(2)}, u32[]{:S(2)}) collective-permute-start(bf16[1024,256]{1,0:T(8,128)(2,1)} %dense_points.1.p0), channel_id=1, source_target_pairs={{0,2},{2,0},{1,3},{3,1},{4,6},{6,4},{5,7},{7,5},{8,10},{10,8},{9,1... | collective-permute-start | bytes 1572872 | tf_op jit(solution)/shard_map/ppermute | solution.py:520
  48.5 22.6 %all-to-all-start.6 = ((f32[8,32,512]{2,1,0:T(8,128)}), f32[8,32,512]{2,1,0:T(8,128)S(1)}, u32[]{:S(2)}, u32[]{:S(2)}) async-start(f32[8,32,512]{2,1,0:T(8,128)} %broadcast_in_dim.27), calls=%async_computation.6 | async-start | bytes 1048576 | tf_op jit(solution)/shard_map/all_to_all | solution.py:501
  52.0 19.1 %collective-permute-start.6 = (bf16[1024,256]{1,0:T(8,128)(2,1)S(1)}, bf16[1024,256]{1,0:T(8,128)(2,1)}, u32[]{:S(2)}, u32[]{:S(2)}) collective-permute-start(bf16[1024,256]{1,0:T(8,128)(2,1)S(1)} %copy-done.1), channel_id=1, source_target_pairs={{0,2},{2,0},{1,3},{3,1},{4,6},{6,4},{5,7},{7,5},{8,10},{10,8},{9,1... | collective-permute-start | bytes 1572872 | tf_op jit(solution)/shard_map/ppermute | solution.py:520
  53.3 29.2 %collective-permute-start.10 = (bf16[1024,256]{1,0:T(8,128)(2,1)}, bf16[1024,256]{1,0:T(8,128)(2,1)}, u32[]{:S(2)}, u32[]{:S(2)}) collective-permute-start(bf16[1024,256]{1,0:T(8,128)(2,1)} %dense_points.1.p0), channel_id=1, source_target_pairs={{0,1},{1,0},{2,3},{3,2},{4,5},{5,4},{6,7},{7,6},{8,9},{9,8},{10,11... | collective-permute-start | bytes 1572872 | tf_op jit(solution)/shard_map/ppermute | solution.py:521
  61.1 21.4 %collective-permute-start.11 = (bf16[1024,256]{1,0:T(8,128)(2,1)}, bf16[1024,256]{1,0:T(8,128)(2,1)}, u32[]{:S(2)}, u32[]{:S(2)}) collective-permute-start(bf16[1024,256]{1,0:T(8,128)(2,1)} %collective-permute-done.9.p1), channel_id=1, source_target_pairs={{0,1},{1,0},{2,3},{3,2},{4,5},{5,4},{6,7},{7,6},{8,9},{9,8},{10,11... | collective-permute-start | bytes 1572872 | tf_op jit(solution)/shard_map/ppermute | solution.py:521
  61.1 68.0 %collective-permute-start.7 = (bf16[1024,256]{1,0:T(8,128)(2,1)S(1)}, bf16[1024,256]{1,0:T(8,128)(2,1)}, u32[]{:S(2)}, u32[]{:S(2)}) collective-permute-start(bf16[1024,256]{1,0:T(8,128)(2,1)S(1)} %copy-done.1), channel_id=1, source_target_pairs={{0,1},{1,0},{2,3},{3,2},{4,5},{5,4},{6,7},{7,6},{8,9},{9,8},{10,11... | collective-permute-start | bytes 1572872 | tf_op jit(solution)/shard_map/ppermute | solution.py:521
  71.1 58.0 %collective-permute-start.8 = (bf16[1024,256]{1,0:T(8,128)(2,1)}, bf16[1024,256]{1,0:T(8,128)(2,1)}, u32[]{:S(2)}, u32[]{:S(2)}) collective-permute-start(bf16[1024,256]{1,0:T(8,128)(2,1)} %collective-permute-done.6.f1), channel_id=1, source_target_pairs={{0,1},{1,0},{2,3},{3,2},{4,5},{5,4},{6,7},{7,6},{8,9},{9,8},{10,11... | collective-permute-start | bytes 1572872 | tf_op jit(solution)/shard_map/ppermute | solution.py:521
  71.1 0.8 copy-start.4
  77.2 59.0 %all-to-all-start.7 = ((f32[8,192,512]{2,1,0:T(8,128)}), f32[8,192,512]{2,1,0:T(8,128)}, u32[]{:S(2)}, u32[]{:S(2)}) async-start(f32[8,192,512]{2,1,0:T(8,128)} %broadcast_in_dim.28), calls=%async_computation.7 | async-start | bytes 6291456 | tf_op jit(solution)/shard_map/all_to_all | solution.py:501
  129.1 7.1 %copy-start.5 = (s32[2,512]{1,0:T(2,128)S(1)}, s32[2,512]{1,0:T(2,128)}, u32[]{:S(2)}) copy-start(s32[2,512]{1,0:T(2,128)} %b_ref.1) | copy-start | bytes 12292
